TPU v7x, 256 devices: a whole 4x4x8 slice. The times are simulated.
256 devices in a mesh: panel: 16 (over z, core), tm: 16 (over x, y).
Axes of the slice: x: 4, y: 4, z: 8, core: 2. Of those that a mesh axis runs over, the one named last changes fastest.
Arguments:
- pressures: bfloat16 [98304, 12288], P('panel', 'tm'), may hold values from -60 to 60
- sketch: bfloat16 [98304, 128], P(('panel', 'tm')), may hold values from -6 to 6
Outputs:
- basis_rows: bfloat16 [12288, 128], P('tm')
- image: float32 [98304, 128], P(('panel', 'tm'))
All inputs are finite; a program needn't handle non-finite values.
Results may differ from a plain program's by a relative error of at most 0.0029.
Values may be sent and summed in bfloat16 or wider, within the bound.
No kernel may reach another device: no remote copies, remote signals or barrier semaphores. Data moves between devices by JAX's collectives and lax.ppermute only.
A program may use at most 64 MiB of HBM per device.

v0:
```python
import jax
import jax.numpy as jnp
from jax import lax
from jax.sharding import PartitionSpec as P


def gram_of(rows_block):
    return lax.dot_general(
        rows_block,
        rows_block,
        (((0,), (0,)), ((), ())),
        precision=lax.Precision.HIGHEST,
        preferred_element_type=jnp.float32,
    )


def orthonormal(rows_block, gram_matrix):
    lower_factor = jnp.linalg.cholesky(gram_matrix)
    solved = jax.scipy.linalg.solve_triangular(lower_factor, rows_block.T, lower=True)
    return solved.T.astype(jnp.bfloat16)


def on_device(pressures, sketch):
    partial_y = lax.dot_general(
        pressures,
        lax.all_gather(sketch, "tm", axis=0, tiled=True),
        (((0,), (0,)), ((), ())),
        preferred_element_type=jnp.float32,
    )
    y_rows = lax.psum(partial_y, "panel")
    gram_matrix = lax.psum(gram_of(y_rows), "tm")
    basis_rows = orthonormal(y_rows, gram_matrix)
    own_rows = pressures.shape[0] // lax.axis_size("tm")
    full_image = lax.psum(jnp.dot(pressures, basis_rows, preferred_element_type=jnp.float32), "tm")
    image = lax.dynamic_slice_in_dim(full_image, lax.axis_index("tm") * own_rows, own_rows, 0)
    return (basis_rows, image)


def solution(mesh):
    return jax.shard_map(
        on_device,
        mesh=mesh,
        in_specs=(P("panel", "tm"), P(("panel", "tm"), None)),
        out_specs=(P("tm", None), P(("panel", "tm"), None)),
        check_vma=False,
    )
```

profile of v0, /device:TPU:8, one launch (start us, length us, event | category | flops | bytes accessed | tf_op | source)
XLA Modules:
  0.0 421.8 jit_solution(15949933175070414837)
XLA Ops:
  7.2 0.0 all-gather.2.cloned.1.call-start
  7.2 0.7 all-gather.2.cloned.1.call-update
  7.9 0.0 all-reduce.4.cloned.1.call-start
  7.9 54.0 %all-gather.2.cloned.1.call-done = bf16[6144,128]{1,0:T(8,128)(2,1)} async-done(((bf16[384,128]{1,0:T(8,128)(2,1)}), bf16[6144,128]{1,0:T(8,128)(2,1)}) %all-gather.2.cloned.1.call-update) | async-done | bytes 1572880 | tf_op jit(solution)/shard_map/all_gather | solution.py:26
  61.9 7.5 %fusion.3 = f32[768,128]{1,0:T(8,128)} fusion(bf16[6144,768]{1,0:T(8,128)(2,1)} %param.2, bf16[6144,128]{1,0:T(8,128)(2,1)} %all-gather.2.cloned.1.call-done), kind=kOutput, calls=%fused_computation.12 | convolution fusion | flops 1207959552 | bytes 11403264 | tf_op jit(solution)/shard_map/dot_general | solution.py:24
  69.4 0.0 all-reduce.4.cloned.1.call-update
  69.4 0.0 all-reduce.6.cloned.1.call-start
  69.5 109.2 %all-reduce.4.cloned.1.call-done = f32[768,128]{1,0:T(8,128)} async-done(((f32[768,128]{1,0:T(8,128)}), f32[768,128]{1,0:T(8,128)}) %all-reduce.4.cloned.1.call-update) | async-done | bytes 393232 | tf_op jit(solution)/shard_map/psum | solution.py:30
  178.7 2.5 fusion.4
  181.2 0.0 all-reduce.6.cloned.1.call-update
  181.2 0.2 all-reduce.8.cloned.1.call-start
  181.5 92.4 %all-reduce.6.cloned.1.call-done = f32[128,128]{0,1:T(8,128)} async-done(((f32[128,128]{0,1:T(8,128)}), f32[128,128]{0,1:T(8,128)}) %all-reduce.6.cloned.1.call-update) | async-done | bytes 65552 | tf_op jit(solution)/shard_map/psum | solution.py:31
  273.8 0.9 copy.5
  274.8 0.9 fusion.2
  275.6 11.7 %cholesky.16 = f32[128,128]{1,0:T(8,128)S(1)} custom-call(f32[128,128]{1,0:T(8,128)S(1)} %fusion.2), custom_call_target="Cholesky" | custom-call | tf_op jit(solution)/shard_map/jit(cholesky)/cholesky | solution.py:18
  287.4 0.6 compare_reduce_fusion
  288.0 0.7 fusion
  288.7 9.8 %custom-call.7 = f32[1,128,128]{1,2,0:T(8,128)S(1)} custom-call(f32[1,128,128]{2,1,0:T(8,128)S(1)} %fusion), custom_call_target="InvertDiagBlocksLowerTriangular" | custom-call | tf_op jit(solution)/shard_map/jit(_solve_triangular)/triangular_solve | solution.py:19
  298.5 1.5 convolution_convert_fusion
  300.0 0.0 copy-start
  300.0 8.7 %convolution_bitcast_fusion = f32[6144,128]{0,1:T(8,128)} fusion(bf16[768,128]{1,0:T(8,128)(2,1)S(1)} %convolution_convert_fusion, bf16[6144,768]{1,0:T(8,128)(2,1)} %param.2), kind=kOutput, calls=%fused_computation | convolution fusion | flops 1207959552 | bytes 12779520 | tf_op jit(solution)/shard_map/dot_general | solution.py:34
  308.6 0.0 copy-done
  308.6 0.0 all-reduce.8.cloned.1.call-update
  308.7 104.9 %all-reduce.8.cloned.1.call-done = f32[6144,128]{0,1:T(8,128)} async-done(((f32[6144,128]{0,1:T(8,128)}), f32[6144,128]{0,1:T(8,128)}) %all-reduce.8.cloned.1.call-update) | async-done | bytes 3145744 | tf_op jit(solution)/shard_map/psum | solution.py:34
  413.5 0.9 constant_dynamic-slice_fusion
  414.5 0.8 copy.6
  (1 shorter events, 0.0 us)
Async XLA Ops:
  7.2 54.8 %all-gather.2.cloned.1.call-start = ((), (), s32[]{:S(2)}) async-start(), calls=%async_computation | async-start | bytes 1671168 | tf_op jit(solution)/shard_map/all_gather | solution.py:26
  7.9 170.8 %all-reduce.4.cloned.1.call-start = ((), (), s32[]{:S(2)}) async-start(), calls=%async_computation.1 | async-start | bytes 786432 | tf_op jit(solution)/shard_map/psum | solution.py:30
  69.4 204.4 %all-reduce.6.cloned.1.call-start = ((), (), s32[]{:S(2)}) async-start(), calls=%async_computation.2 | async-start | bytes 131072 | tf_op jit(solution)/shard_map/psum | solution.py:31
  181.2 232.3 %all-reduce.8.cloned.1.call-start = ((), (), s32[]{:S(2)}) async-start(), calls=%async_computation.3 | async-start | bytes 6291456 | tf_op jit(solution)/shard_map/psum | solution.py:34
  300.0 8.7 %copy-start = (bf16[768,128]{1,0:T(8,128)(2,1)}, bf16[768,128]{1,0:T(8,128)(2,1)S(1)}, u32[]{:S(2)}) copy-start(bf16[768,128]{1,0:T(8,128)(2,1)S(1)} %convolution_convert_fusion) | copy-start | bytes 589828
Sparse Core Ops, SparseCore 0:
  10.5 51.4 all-gather.1
  69.6 109.0 all-reduce.3
  182.8 91.0 all-reduce.5
  308.8 104.6 all-reduce.7
where the time goes:
time: 424 us; the launch traced here: 422 us
  waiting for transfers between devices  361 us (85%)
  other arithmetic  23.7 us (6%)
  matrix products  20.1 us (5%)
  between operations  13.8 us (3%)
    psum x1, waiting for transfers between devices, on_device(): y_rows = lax.psum(partial_y, 'panel')  109 us
    psum x1, waiting for transfers between devices, on_device(): lax.psum(jnp.dot(pressures, basis_rows, preferred_element_type=jnp.float3...  105 us
    psum x1, waiting for transfers between devices, on_device(): gram_matrix = lax.psum(gram_of(y_rows), 'tm')  92.4 us
    all_gather x1, waiting for transfers between devices, on_device(): lax.all_gather(sketch, 'tm', axis=0, tiled=True)  54 us
    another operation x3, other arithmetic, orthonormal(): lower_factor = jnp.linalg.cholesky(gram_matrix)  12.4 us
    another operation x2, other arithmetic, orthonormal(): jax.scipy.linalg.solve_triangular(lower_factor, rows_block.T, lower=True)  10.5 us
    dot_general x1, matrix products, on_device(): jnp.dot(pressures, basis_rows, preferred_element_type=jnp.float32)  8.66 us
  transfers between devices with their start and end apart: 4, of which 4 were waited for; matrix products, arithmetic and copies ran while one was open for 0% of the time, Pallas kernels for 0%

commit v1 on v0

v1 whole, which is shorter than its diff:
```python
import jax
import jax.numpy as jnp
from jax import lax
from jax.sharding import PartitionSpec as P

F32 = jnp.float32
BF16 = jnp.bfloat16


def spread(block, axis):
    size = lax.axis_size(axis)
    return lax.all_to_all(jnp.broadcast_to(block[None], (size, *block.shape)), axis, 0, 0)


def sum_scattered(rows, axis, sent_as):
    size = lax.axis_size(axis)
    parts = rows.reshape(size, rows.shape[0] // size, rows.shape[1]).astype(sent_as)
    return jnp.sum(lax.all_to_all(parts, axis, 0, 0).astype(F32), axis=0)


def gram_of(rows_block):
    return lax.dot_general(
        rows_block,
        rows_block,
        (((0,), (0,)), ((), ())),
        precision=lax.Precision.HIGHEST,
        preferred_element_type=F32,
    )


def gram_summed(y_rows):
    partial = gram_of(y_rows)
    modes = partial.shape[0]
    core = lax.axis_index("panel") % 2
    half = lax.dynamic_slice_in_dim(partial, core * (modes // 2), modes // 2, 0)
    mine = jnp.sum(spread(half, "tm"), axis=0)
    other = lax.ppermute(mine, "panel", [(i, i ^ 1) for i in range(lax.axis_size("panel"))])
    low = jnp.where(core == 0, mine, other)
    high = jnp.where(core == 0, other, mine)
    return jnp.concatenate([low, high], axis=0)


def orthonormal(rows_block, gram_matrix):
    lower_factor = jnp.linalg.cholesky(gram_matrix)
    solved = jax.scipy.linalg.solve_triangular(lower_factor, rows_block.T, lower=True)
    return solved.T.astype(BF16)


def on_device(pressures, sketch):
    panels, samples = pressures.shape
    modes = sketch.shape[1]
    partial_y = lax.dot_general(
        pressures,
        spread(sketch, "tm").reshape(panels, modes),
        (((0,), (0,)), ((), ())),
        preferred_element_type=F32,
    )
    y_rows = spread(sum_scattered(partial_y, "panel", F32), "panel").reshape(samples, modes)
    basis_rows = orthonormal(y_rows, gram_summed(y_rows))
    partial_image = jnp.dot(pressures, basis_rows, preferred_element_type=F32)
    image = sum_scattered(partial_image, "tm", BF16)
    return (basis_rows, image)


def solution(mesh):
    return jax.shard_map(
        on_device,
        mesh=mesh,
        in_specs=(P("panel", "tm"), P(("panel", "tm"), None)),
        out_specs=(P("tm", None), P(("panel", "tm"), None)),
        check_vma=False,
    )
```

time: 424 us -> 157 us (0.37)
  waiting for transfers between devices: 361 us -> 24.6 us
  blocking collectives: 0 us -> 65 us
  local copies, waits for them, and re-layouts: 2.68 us -> 17.1 us
  between operations: 13.8 us -> 0.78 us
  starting transfers between devices: 0.34 us -> 11.5 us
  matrix products: 20.1 us -> 13.4 us
    psum x3 -> x0, waiting for transfers between devices: 306 us -> none  [the longest x1 109 us: on_device(): y_rows = lax.psum(partial_y, 'panel')]
    all_to_all x0 -> x3, blocking collectives: none -> 65 us  [the longest x2 48.4 us: sum_scattered(): return jnp.sum(lax.all_to_all(parts, axis, 0, 0).astype(F32), axis=0)]
    all_gather x1 -> x0, waiting for transfers between devices: 54 us -> none  [on_device(): lax.all_gather(sketch, 'tm', axis=0, tiled=True)]
    all_to_all x0 -> x2, waiting for transfers between devices: none -> 23.5 us  [spread(): lax.all_to_all(jnp.broadcast_to(block[None], (size, *block.shape)), axis,...]
    unnamed x3 -> x4, local copies, waits for them, and re-layouts: 0.82 us -> 13.5 us
    all_to_all x0 -> x2, starting transfers between devices: none -> 11.1 us  [spread(): lax.all_to_all(jnp.broadcast_to(block[None], (size, *block.shape)), axis,...]
  transfers between devices with their start and end apart: 4 -> 3, of which waited for: 4 -> 3; matrix products, arithmetic and copies ran while one was open for 0% -> 8% of each run, Pallas kernels for 0% -> 0%
where the time goes in v1:
time: 157 us; the launch traced here: 156 us
  blocking collectives  65 us (41%)
  waiting for transfers between devices  24.6 us (16%)
  other arithmetic  23.3 us (15%)
  local copies, waits for them, and re-layouts  17.1 us (11%)
  matrix products  13.4 us (9%)
  starting transfers between devices  11.5 us (7%)
    all_to_all x2, blocking collectives, sum_scattered(): return jnp.sum(lax.all_to_all(parts, axis, 0, 0).astype(F32), axis=0)  48.4 us
    all_to_all x2, waiting for transfers between devices, spread(): lax.all_to_all(jnp.broadcast_to(block[None], (size, *block.shape)), axis,...  23.5 us
    all_to_all x1, blocking collectives, spread(): lax.all_to_all(jnp.broadcast_to(block[None], (size, *block.shape)), axis,...  16.6 us
    unnamed x4, local copies, waits for them, and re-layouts  13.5 us
    another operation x3, other arithmetic, orthonormal(): lower_factor = jnp.linalg.cholesky(gram_matrix)  12.4 us
    all_to_all x2, starting transfers between devices, spread(): lax.all_to_all(jnp.broadcast_to(block[None], (size, *block.shape)), axis,...  11.1 us
    another operation x2, other arithmetic, orthonormal(): jax.scipy.linalg.solve_triangular(lower_factor, rows_block.T, lower=True)  10.5 us
    dot_general x1, matrix products, on_device(): partial_image = jnp.dot(pressures, basis_rows, preferred_element_type=F32)  6.95 us
  transfers between devices with their start and end apart: 3, of which 3 were waited for; matrix products, arithmetic and copies ran while one was open for 8% of the time, Pallas kernels for 0%

profile of v1, /device:TPU:8, one launch (start us, length us, event | category | flops | bytes accessed | tf_op | source)
XLA Modules:
  0.0 155.7 jit_solution(6394254727835924541)
XLA Ops:
  0.6 2.4 %broadcast_in_dim.7 = bf16[16,384,128]{2,1,0:T(8,128)(2,1)} broadcast(bf16[384,128]{1,0:T(8,128)(2,1)} %param.3), dimensions={1,2} | broadcast | bytes 1671168 | tf_op jit(solution)/shard_map/broadcast_in_dim | solution.py:12
  3.0 7.4 %all-to-all-start = ((bf16[16,384,128]{2,1,0:T(8,128)(2,1)}), bf16[16,384,128]{2,1,0:T(8,128)(2,1)S(1)}, u32[]{:S(2)}, u32[]{:S(2)}) async-start(bf16[16,384,128]{2,1,0:T(8,128)(2,1)} %broadcast_in_dim.7), calls=%async_computation | async-start | bytes 3145728 | tf_op jit(solution)/shard_map/all_to_all | solution.py:12
  10.4 12.7 %copy.13 = bf16[6144,768]{0,1:T(8,128)(2,1)} copy(bf16[6144,768]{1,0:T(8,128)(2,1)} %param.2) | data formatting | bytes 18874368 | tf_op args[0]
  23.1 9.7 %all-to-all-done = bf16[16,384,128]{2,1,0:T(8,128)(2,1)S(1)} async-done(((bf16[16,384,128]{2,1,0:T(8,128)(2,1)}), bf16[16,384,128]{2,1,0:T(8,128)(2,1)S(1)}, u32[]{:S(2)}, u32[]{:S(2)}) %all-to-all-start) | async-done | bytes 1572896 | tf_op jit(solution)/shard_map/all_to_all | solution.py:12
  32.8 5.2 %fusion.3 = f32[16,48,128]{2,1,0:T(8,128)S(1)} fusion(bf16[16,48,6144]{2,1,0:T(8,128)(2,1)} %bitcast.30, bf16[6144,128,1]{1,0,2:T(8,128)(2,1)S(1)} %bitcast.34), kind=kOutput, calls=%fused_computation.18 | convolution fusion | flops 1207959552 | bytes 11403264 | tf_op jit(solution)/shard_map/dot_general | solution.py:52
  38.0 22.1 %all_to_all.25 = f32[16,48,128]{2,1,0:T(8,128)S(1)} all-to-all(f32[16,48,128]{2,1,0:T(8,128)S(1)} %fusion.3), channel_id=1, replica_groups=mesh['panel'=16,'tm'=16] {'panel'}, dimensions={0} | all-to-all | bytes 786432 | tf_op jit(solution)/shard_map/all_to_all | solution.py:18
  60.1 0.8 broadcast_in_dim.8
  60.8 3.7 %all-to-all-start.2 = ((f32[16,48,128]{2,1,0:T(8,128)}), f32[16,48,128]{2,1,0:T(8,128)S(1)}, u32[]{:S(2)}, u32[]{:S(2)}) async-start(f32[16,48,128]{2,1,0:T(8,128)} %broadcast_in_dim.8), calls=%async_computation.2 | async-start | bytes 786432 | tf_op jit(solution)/shard_map/all_to_all | solution.py:12
  64.6 13.7 %all-to-all-done.2 = f32[16,48,128]{2,1,0:T(8,128)S(1)} async-done(((f32[16,48,128]{2,1,0:T(8,128)}), f32[16,48,128]{2,1,0:T(8,128)S(1)}, u32[]{:S(2)}, u32[]{:S(2)}) %all-to-all-start.2) | async-done | bytes 393248 | tf_op jit(solution)/shard_map/all_to_all | solution.py:12
  78.3 0.8 convolution_bitcast_fusion
  79.2 16.6 %all_to_all.26 = f32[16,64,128]{2,1,0:T(8,128)S(1)} all-to-all(f32[16,64,128]{2,1,0:T(8,128)S(1)} %broadcast_in_dim.9), channel_id=1, replica_groups=mesh['panel'=16,'tm'=16] {'tm'}, dimensions={0} | all-to-all | bytes 1048576 | tf_op jit(solution)/shard_map/all_to_all | solution.py:12
  95.8 0.1 copy.15
  95.9 0.4 collective-permute-start
  96.3 1.2 collective-permute-done
  97.4 0.1 pad_maximum_fusion
  97.5 0.1 copy.17
  97.6 0.1 fusion.2
  97.7 11.7 %cholesky.16 = f32[128,128]{1,0:T(8,128)S(1)} custom-call(f32[128,128]{1,0:T(8,128)S(1)} %fusion.2), custom_call_target="Cholesky" | custom-call | tf_op jit(solution)/shard_map/jit(cholesky)/cholesky | solution.py:44
  109.5 0.6 compare_reduce_fusion
  110.1 0.7 fusion
  110.8 9.8 %custom-call.7 = f32[1,128,128]{1,2,0:T(8,128)S(1)} custom-call(f32[1,128,128]{2,1,0:T(8,128)S(1)} %fusion), custom_call_target="InvertDiagBlocksLowerTriangular" | custom-call | tf_op jit(solution)/shard_map/jit(_solve_triangular)/triangular_solve | solution.py:45
  120.6 0.5 convolution_convert_fusion.1
  121.1 0.0 copy-start
  121.1 7.0 %convolution_convert_fusion = bf16[128,6144]{1,0:T(8,128)(2,1)S(1)} fusion(bf16[768,128]{1,0:T(8,128)(2,1)S(1)} %convolution_convert_fusion.1, bf16[6144,768]{1,0:T(8,128)(2,1)} %param.2), kind=kOutput, calls=%fused_computation | convolution fusion | flops 1208745984 | bytes 11206656 | tf_op jit(solution)/shard_map/dot_general | solution.py:60
  128.0 0.0 copy-done
  128.0 0.2 copy.24
  128.3 26.4 %all_to_all.27 = bf16[16,384,128]{1,2,0:T(8,128)(2,1)S(1)} all-to-all(bf16[16,384,128]{1,2,0:T(8,128)(2,1)S(1)} %bitcast.31), channel_id=1, replica_groups=mesh['panel'=16,'tm'=16] {'tm'}, dimensions={0} | all-to-all | bytes 3145728 | tf_op jit(solution)/shard_map/all_to_all | solution.py:18
  154.7 0.2 convert_reduce_fusion
  154.9 0.8 copy.20
  (6 shorter events, 0.2 us)
Async XLA Ops:
  3.0 29.8 %all-to-all-start = ((bf16[16,384,128]{2,1,0:T(8,128)(2,1)}), bf16[16,384,128]{2,1,0:T(8,128)(2,1)S(1)}, u32[]{:S(2)}, u32[]{:S(2)}) async-start(bf16[16,384,128]{2,1,0:T(8,128)(2,1)} %broadcast_in_dim.7), calls=%async_computation | async-start | bytes 3145728 | tf_op jit(solution)/shard_map/all_to_all | solution.py:12
  60.8 17.5 %all-to-all-start.2 = ((f32[16,48,128]{2,1,0:T(8,128)}), f32[16,48,128]{2,1,0:T(8,128)S(1)}, u32[]{:S(2)}, u32[]{:S(2)}) async-start(f32[16,48,128]{2,1,0:T(8,128)} %broadcast_in_dim.8), calls=%async_computation.2 | async-start | bytes 786432 | tf_op jit(solution)/shard_map/all_to_all | solution.py:12
  95.9 1.5 collective-permute-start
  121.1 7.0 %copy-start = (bf16[768,128]{1,0:T(8,128)(2,1)}, bf16[768,128]{1,0:T(8,128)(2,1)S(1)}, u32[]{:S(2)}) copy-start(bf16[768,128]{1,0:T(8,128)(2,1)S(1)} %convolution_convert_fusion.1) | copy-start | bytes 589828

commit v2 on v0

v2 whole, which is shorter than its diff:
```python
import jax
import jax.numpy as jnp
from jax import lax
from jax.experimental import pallas as pl
from jax.experimental.pallas import tpu as pltpu
from jax.sharding import PartitionSpec as P

F32 = jnp.float32
BF16 = jnp.bfloat16
GROUP = 8
PIECES = 6
IN_HBM = pl.BlockSpec(memory_space=pltpu.HBM)
IN_VMEM = pl.BlockSpec(memory_space=pltpu.VMEM)
ROOM = pltpu.CompilerParams(vmem_limit_bytes=32 << 20)


def spread(block, axis):
    size = lax.axis_size(axis)
    return lax.all_to_all(jnp.broadcast_to(block[None], (size, *block.shape)), axis, 0, 0)


def fetch(pressures, held, arrived):
    rows = held.shape[0] // PIECES
    parts = [pl.ds(i * rows, rows) for i in range(PIECES)]
    copies = [pltpu.make_async_copy(pressures.at[r], held.at[r], arrived.at[i]) for i, r in enumerate(parts)]
    for copy in copies:
        copy.start()
    return list(zip(copies, parts))


def held_like(pressures):
    return [pltpu.VMEM(pressures.shape, pressures.dtype), pltpu.SemaphoreType.DMA((PIECES,))]


def projection_kernel(pressures, sketch, y_ref, held, arrived):
    total = None
    for copy, r in fetch(pressures, held, arrived):
        copy.wait()
        term = lax.dot_general(sketch[r, :], held[r, :], (((0,), (0,)), ((), ())), preferred_element_type=F32)
        total = term if total is None else total + term
    y_ref[...] = total.T


def projection(pressures, sketch):
    panels, samples = pressures.shape
    modes = sketch.shape[1]
    return pl.pallas_call(
        projection_kernel,
        out_shape=jax.ShapeDtypeStruct((samples, modes), F32),
        in_specs=[IN_HBM, IN_VMEM],
        out_specs=IN_VMEM,
        scratch_shapes=held_like(pressures),
        compiler_params=ROOM,
    )(pressures, sketch)


def inverse_factor(gram):
    n = gram.shape[0]
    groups = n // GROUP
    sub = lax.broadcasted_iota(jnp.int32, (GROUP, n), 0)
    lane = lax.broadcasted_iota(jnp.int32, (GROUP, n), 1)

    def wide(x):
        return jnp.broadcast_to(x, (GROUP, n))

    left = [gram[GROUP * i : GROUP * (i + 1), :] for i in range(groups)]
    right = [jnp.where(lane == sub + GROUP * i, 1.0, 0.0).astype(F32) for i in range(groups)]
    steps = range(GROUP)
    for g in range(groups):
        k = GROUP * g
        columns = [wide(left[g][:, k + m : k + m + 1]) for m in steps]
        block = {(m, l): columns[l][m : m + 1, :] for m in steps for l in range(m, GROUP)}
        over, scale = [], {}
        for m in steps:
            over.append(1.0 / block[m, m])
            for l in range(m + 1, GROUP):
                scale[m, l] = block[m, l] * over[m]
            for p in range(m + 1, GROUP):
                for l in range(p, GROUP):
                    block[p, l] = block[p, l] - scale[m, p] * block[m, l]
        rows_left, rows_right = [], []
        for m in steps:
            a, b = left[g][m : m + 1, :], right[g][m : m + 1, :]
            for l in range(m):
                a = a - scale[l, m] * rows_left[l]
                b = b - scale[l, m] * rows_right[l]
            rows_left.append(a)
            rows_right.append(b)
        pivot_left = [wide(rows_left[m] * over[m]) for m in steps]
        pivot_right = [wide(rows_right[m] * over[m]) for m in steps]
        scales = {key: wide(value) for key, value in scale.items()}
        for i in range(g, groups):
            own = i == g
            entries = columns if own else [wide(left[i][:, k + m : k + m + 1]) for m in steps]
            factors = []
            for m in steps:
                f = entries[m]
                for l in range(m):
                    f = f - scales[l, m] * factors[l]
                factors.append(f)
            a, b = left[i], right[i]
            for m in range(GROUP - 1) if own else steps:
                f = jnp.where(sub > m, factors[m], 0.0) if own else factors[m]
                a = a - f * pivot_left[m]
                b = b - f * pivot_right[m]
            left[i], right[i] = a, b
    out = []
    for i in range(groups):
        pivots = jnp.sum(jnp.where(lane == sub + GROUP * i, left[i], 0.0), axis=1, keepdims=True)
        root = lax.rsqrt(pivots)
        root = root * (1.5 - 0.5 * pivots * root * root)
        out.append(right[i] * root)
    return out


def image_kernel(core, pressures, mine, other, y_ref, basis_ref, image_ref, held, arrived, inverse):
    arriving = fetch(pressures, held, arrived)
    first = core[0] == 0
    low = jnp.where(first, mine[...], other[...])
    high = jnp.where(first, other[...], mine[...])
    for i, rows in enumerate(inverse_factor(jnp.concatenate([low, high], axis=0))):
        inverse[GROUP * i : GROUP * (i + 1), :] = rows
    basis = lax.dot_general(
        y_ref[...],
        inverse[...],
        (((1,), (1,)), ((), ())),
        precision=lax.Precision.HIGHEST,
        preferred_element_type=F32,
    ).astype(BF16)
    basis_ref[...] = basis
    for copy, r in arriving:
        copy.wait()
        image_ref[r, :] = jnp.dot(held[r, :], basis, preferred_element_type=F32).astype(BF16)


def basis_and_image(core, pressures, mine, other, y_rows):
    panels = pressures.shape[0]
    samples, modes = y_rows.shape
    return pl.pallas_call(
        image_kernel,
        out_shape=(
            jax.ShapeDtypeStruct((samples, modes), BF16),
            jax.ShapeDtypeStruct((panels, modes), BF16),
        ),
        in_specs=[pl.BlockSpec(memory_space=pltpu.SMEM), IN_HBM, IN_VMEM, IN_VMEM, IN_VMEM],
        out_specs=(IN_VMEM, IN_VMEM),
        scratch_shapes=[*held_like(pressures), pltpu.VMEM((modes, modes), F32)],
        compiler_params=ROOM,
    )(core[None], pressures, mine, other, y_rows)


def gram_half(y_rows, core):
    gram = lax.dot_general(
        y_rows,
        y_rows,
        (((0,), (0,)), ((), ())),
        precision=lax.Precision.HIGHEST,
        preferred_element_type=F32,
    )
    half = gram.shape[0] // 2
    return lax.dynamic_slice_in_dim(gram, core * half, half, 0)


def on_device(pressures, sketch):
    pressures = pltpu.with_memory_space_constraint(pressures, pltpu.HBM)
    panels, samples = pressures.shape
    modes = sketch.shape[1]
    across = lax.axis_size("panel")
    core = lax.axis_index("panel") % 2
    partial_y = projection(pressures, spread(sketch, "tm").reshape(panels, modes))
    pieces = lax.all_to_all(partial_y.reshape(across, samples // across, modes), "panel", 0, 0)
    y_rows = spread(jnp.sum(pieces, axis=0), "panel").reshape(samples, modes)
    mine = jnp.sum(spread(gram_half(y_rows, core), "tm"), axis=0)
    other = lax.ppermute(mine, "panel", [(i, i ^ 1) for i in range(across)])
    basis_rows, partial_image = basis_and_image(core, pressures, mine, other, y_rows)
    parts = lax.all_to_all(partial_image.reshape(lax.axis_size("tm"), -1, modes), "tm", 0, 0)
    image = jnp.sum(parts.astype(F32), axis=0)
    return (basis_rows, image)


def solution(mesh):
    return jax.shard_map(
        on_device,
        mesh=mesh,
        in_specs=(P("panel", "tm"), P(("panel", "tm"), None)),
        out_specs=(P("tm", None), P(("panel", "tm"), None)),
        check_vma=False,
    )
```

time: 424 us -> 132 us (0.31)
  waiting for transfers between devices: 361 us -> 14.9 us
  blocking collectives: 0 us -> 93.4 us
  other arithmetic: 23.7 us -> 0.96 us
  matrix products: 20.1 us -> 0.8 us
  Pallas kernels: 0 us -> 14.4 us
  between operations: 13.8 us -> 0.7 us
    psum x3 -> x0, waiting for transfers between devices: 306 us -> none  [the longest x1 109 us: on_device(): y_rows = lax.psum(partial_y, 'panel')]
    all_to_all x0 -> x4, blocking collectives: none -> 93.4 us  [the longest x2 44.9 us: spread(): lax.all_to_all(jnp.broadcast_to(block[None], (size, *block.shape)), axis,...]
    all_gather x1 -> x0, waiting for transfers between devices: 54 us -> none  [on_device(): lax.all_gather(sketch, 'tm', axis=0, tiled=True)]
    another operation x5 -> x0, other arithmetic: 22.9 us -> none  [the longest x3 12.4 us: orthonormal(): lower_factor = jnp.linalg.cholesky(gram_matrix)]
    dot_general x3 -> x1, matrix products: 18.7 us -> 0.8 us  [gram_half(): lax.dot_general(y_rows, y_rows, (((0,), (0,)), ((), ())), precision=lax.P...]
    pallas_call x0 -> x2, Pallas kernels: none -> 14.4 us  [the longest x1 10.1 us: basis_and_image(): pl.pallas_call(image_kernel, out_shape=(jax.ShapeDtypeStruct((samples, mo...]
    all_to_all x0 -> x1, waiting for transfers between devices: none -> 13.7 us  [spread(): lax.all_to_all(jnp.broadcast_to(block[None], (size, *block.shape)), axis,...]
  transfers between devices with their start and end apart: 4 -> 2, of which waited for: 4 -> 2; matrix products, arithmetic and copies ran while one was open for 0% -> 0% of each run, Pallas kernels for 0% -> 0%
where the time goes in v2:
time: 132 us; the launch traced here: 131 us
  blocking collectives  93.4 us (71%)
  waiting for transfers between devices  14.9 us (11%)
  Pallas kernels  14.4 us (11%)
  starting transfers between devices  3.9 us (3%)
  local copies, waits for them, and re-layouts  2.01 us (2%)
    all_to_all x2, blocking collectives, spread(): lax.all_to_all(jnp.broadcast_to(block[None], (size, *block.shape)), axis,...  44.9 us
    all_to_all x1, blocking collectives, on_device(): lax.all_to_all(partial_image.reshape(lax.axis_size('tm'), -1, modes), 'tm...  26.4 us
    all_to_all x1, blocking collectives, on_device(): lax.all_to_all(partial_y.reshape(across, samples // across, modes), 'pane...  22.1 us
    all_to_all x1, waiting for transfers between devices, spread(): lax.all_to_all(jnp.broadcast_to(block[None], (size, *block.shape)), axis,...  13.7 us
    pallas_call x1, Pallas kernels, basis_and_image(): pl.pallas_call(image_kernel, out_shape=(jax.ShapeDtypeStruct((samples, mo...  10.1 us
    pallas_call x1, Pallas kernels, projection(): pl.pallas_call(projection_kernel, out_shape=jax.ShapeDtypeStruct((samples...  4.32 us
    all_to_all x1, starting transfers between devices, spread(): lax.all_to_all(jnp.broadcast_to(block[None], (size, *block.shape)), axis,...  3.72 us
  transfers between devices with their start and end apart: 2, of which 2 were waited for; matrix products, arithmetic and copies ran while one was open for 0% of the time, Pallas kernels for 0%

profile of v2, /device:TPU:8, one launch (start us, length us, event | category | flops | bytes accessed | tf_op | source)
XLA Modules:
  0.0 131.0 jit_solution(16243344701525820370)
XLA Ops:
  0.6 1.2 broadcast_in_dim.9
  1.8 28.2 %all_to_all.25 = bf16[16,384,128]{2,1,0:T(8,128)(2,1)S(1)} all-to-all(bf16[16,384,128]{2,1,0:T(8,128)(2,1)S(1)} %broadcast_in_dim.9), channel_id=1, replica_groups=mesh['panel'=16,'tm'=16] {'tm'}, dimensions={0} | all-to-all | bytes 3145728 | tf_op jit(solution)/shard_map/all_to_all | solution.py:19
  30.0 4.3 %shard_map.41 = f32[768,128]{1,0:T(8,128)S(1)} custom-call(bf16[6144,768]{1,0:T(8,128)(2,1)} %pressures.3, bf16[6144,128]{1,0:T(8,128)(2,1)S(1)} %bitcast.10), custom_call_target="tpu_custom_call" | custom-call | tf_op jit(solution)/shard_map/pallas_call | solution.py:47
  34.4 22.1 %all_to_all.26 = f32[16,48,128]{2,1,0:T(8,128)S(1)} all-to-all(f32[16,48,128]{2,1,0:T(8,128)S(1)} %bitcast.11), channel_id=1, replica_groups=mesh['panel'=16,'tm'=16] {'panel'}, dimensions={0} | all-to-all | bytes 786432 | tf_op jit(solution)/shard_map/all_to_all | solution.py:171
  56.4 0.8 broadcast_in_dim.10
  57.2 3.7 %all-to-all-start.2 = ((f32[16,48,128]{2,1,0:T(8,128)}), f32[16,48,128]{2,1,0:T(8,128)S(1)}, u32[]{:S(2)}, u32[]{:S(2)}) async-start(f32[16,48,128]{2,1,0:T(8,128)} %broadcast_in_dim.10), calls=%async_computation.2 | async-start | bytes 786432 | tf_op jit(solution)/shard_map/all_to_all | solution.py:19
  61.0 13.7 %all-to-all-done.2 = f32[16,48,128]{2,1,0:T(8,128)S(1)} async-done(((f32[16,48,128]{2,1,0:T(8,128)}), f32[16,48,128]{2,1,0:T(8,128)S(1)}, u32[]{:S(2)}, u32[]{:S(2)}) %all-to-all-start.2) | async-done | bytes 393248 | tf_op jit(solution)/shard_map/all_to_all | solution.py:19
  74.7 0.8 convolution_bitcast_fusion
  75.6 16.7 %all_to_all.27 = f32[16,64,128]{2,1,0:T(8,128)S(1)} all-to-all(f32[16,64,128]{2,1,0:T(8,128)S(1)} %broadcast_in_dim.11), channel_id=1, replica_groups=mesh['panel'=16,'tm'=16] {'tm'}, dimensions={0} | all-to-all | bytes 1048576 | tf_op jit(solution)/shard_map/all_to_all | solution.py:19
  92.3 0.2 collective-permute-start
  92.5 1.1 collective-permute-done.other
  93.6 10.1 %shard_map.42 = (bf16[768,128]{1,0:T(8,128)(2,1)}, bf16[6144,128]{1,0:T(8,128)(2,1)S(1)}) custom-call(s32[1]{0:T(128)} %bitcast.core, bf16[6144,768]{1,0:T(8,128)(2,1)} %pressures.3, f32[64,128]{1,0:T(8,128)S(1)} %reduce_sum.28.mine, f32[64,128]{1,0:T(8,128)S(1)} %collective-permute-done.other, f32[768,128]{1,0:T(8,128)S(1)} %bitcast.9), custom_call_target="tpu_custom_call" | custom-call | tf_op jit(solution)/shard_map/pallas_call | solution.py:139
  103.7 26.4 %all_to_all.28 = bf16[16,384,128]{2,1,0:T(8,128)(2,1)S(1)} all-to-all(bf16[16,384,128]{2,1,0:T(8,128)(2,1)S(1)} %bitcast.12), channel_id=1, replica_groups=mesh['panel'=16,'tm'=16] {'tm'}, dimensions={0} | all-to-all | bytes 3145728 | tf_op jit(solution)/shard_map/all_to_all | solution.py:176
  130.1 0.9 convert_reduce_fusion
  (4 shorter events, 0.1 us)
Async XLA Ops:
  57.2 17.5 %all-to-all-start.2 = ((f32[16,48,128]{2,1,0:T(8,128)}), f32[16,48,128]{2,1,0:T(8,128)S(1)}, u32[]{:S(2)}, u32[]{:S(2)}) async-start(f32[16,48,128]{2,1,0:T(8,128)} %broadcast_in_dim.10), calls=%async_computation.2 | async-start | bytes 786432 | tf_op jit(solution)/shard_map/all_to_all | solution.py:19
  92.3 1.3 collective-permute-start

commit v3 on v2

v3 whole, which is shorter than its diff:
```python
import jax
import jax.numpy as jnp
from jax import lax
from jax.experimental import pallas as pl
from jax.experimental.pallas import tpu as pltpu
from jax.sharding import PartitionSpec as P

F32 = jnp.float32
BF16 = jnp.bfloat16
GROUP = 8
PIECES = 6
IN_HBM = pl.BlockSpec(memory_space=pltpu.HBM)
IN_VMEM = pl.BlockSpec(memory_space=pltpu.VMEM)
ROOM = pltpu.CompilerParams(vmem_limit_bytes=32 << 20)


def fetch(pressures, held, arrived):
    rows = held.shape[0] // PIECES
    parts = [pl.ds(i * rows, rows) for i in range(PIECES)]
    copies = [pltpu.make_async_copy(pressures.at[r], held.at[r], arrived.at[i]) for i, r in enumerate(parts)]
    for copy in copies:
        copy.start()
    return list(zip(copies, parts))


def held_like(pressures):
    return [pltpu.VMEM(pressures.shape, pressures.dtype), pltpu.SemaphoreType.DMA((PIECES,))]


def own_core():
    return lax.rem(lax.axis_index("panel"), 2)


def projection_kernel(pressures, sketch, keep_ref, give_ref, held, arrived):
    total = None
    for copy, r in fetch(pressures, held, arrived):
        copy.wait()
        term = lax.dot_general(sketch[r, :], held[r, :], (((0,), (0,)), ((), ())), preferred_element_type=F32)
        total = term if total is None else total + term
    chips, rows, modes = keep_ref.shape
    y = total.T.reshape(chips, 2, rows, modes)
    first = own_core() == 0
    keep_ref[...] = jnp.where(first, y[:, 0], y[:, 1])
    give_ref[...] = jnp.where(first, y[:, 1], y[:, 0])


def projection(pressures, sketch, chips):
    samples = pressures.shape[1]
    modes = sketch.shape[1]
    half = jax.ShapeDtypeStruct((chips, samples // (2 * chips), modes), F32)
    return pl.pallas_call(
        projection_kernel,
        out_shape=(half, half),
        in_specs=[IN_HBM, IN_VMEM],
        out_specs=(IN_VMEM, IN_VMEM),
        scratch_shapes=held_like(pressures),
        compiler_params=ROOM,
    )(pressures, sketch)


def gram_kernel(mine, other, y_ref, half_ref):
    first = own_core() == 0
    y_ref[:, 0] = jnp.where(first, mine[...], other[...])
    y_ref[:, 1] = jnp.where(first, other[...], mine[...])
    copies, half, modes = half_ref.shape
    y = y_ref[...].reshape(-1, modes)
    gram = lax.dot_general(
        y, y, (((0,), (0,)), ((), ())), precision=lax.Precision.HIGHEST, preferred_element_type=F32
    )
    half_ref[...] = jnp.broadcast_to(jnp.where(first, gram[:half], gram[half:])[None], half_ref.shape)


def rows_and_gram(mine, other, copies):
    chips, rows, modes = mine.shape
    return pl.pallas_call(
        gram_kernel,
        out_shape=(
            jax.ShapeDtypeStruct((chips, 2, rows, modes), F32),
            jax.ShapeDtypeStruct((copies, modes // 2, modes), F32),
        ),
        in_specs=[IN_VMEM, IN_VMEM],
        out_specs=(IN_VMEM, IN_VMEM),
        compiler_params=ROOM,
    )(mine, other)


def inverse_factor(gram):
    n = gram.shape[0]
    groups = n // GROUP
    sub = lax.broadcasted_iota(jnp.int32, (GROUP, n), 0)
    lane = lax.broadcasted_iota(jnp.int32, (GROUP, n), 1)
    steps = range(GROUP)

    def wide(x):
        return jnp.broadcast_to(x, (GROUP, n))

    def columns_of(rows, k):
        return [wide(rows[:, k + m : k + m + 1]) for m in steps]

    left = [gram[GROUP * i : GROUP * (i + 1), :] for i in range(groups)]
    out = []
    for g in range(groups):
        k = GROUP * g
        inside = (lane >= k) & (lane < k + GROUP)
        columns = columns_of(left[g], k)
        block = {(m, l): columns[l][m : m + 1, :] for m in steps for l in range(m, GROUP)}
        over, scale = [], {}
        for m in steps:
            over.append(1.0 / block[m, m])
            for l in range(m + 1, GROUP):
                scale[m, l] = block[m, l] * over[m]
            for p in range(m + 1, GROUP):
                for l in range(p, GROUP):
                    block[p, l] = block[p, l] - scale[m, p] * block[m, l]
        start = jnp.where(inside, jnp.where(lane == sub + k, 1.0, 0.0), left[g])
        rows = []
        for m in steps:
            row = start[m : m + 1, :]
            for l in range(m):
                row = row - scale[l, m] * rows[l]
            rows.append(row)
        pivots = [wide(rows[m] * over[m]) for m in steps]
        scales = {key: wide(value) for key, value in scale.items()}
        for i in range(g + 1, groups):
            factors = []
            for m, f in enumerate(columns_of(left[i], k)):
                for l in range(m):
                    f = f - scales[l, m] * factors[l]
                factors.append(f)
            rest = jnp.where(inside, 0.0, left[i])
            for f, pivot in zip(factors, pivots):
                rest = rest - f * pivot
            left[i] = rest
        scaled = []
        for m in steps:
            root = lax.rsqrt(block[m, m])
            scaled.append(rows[m] * (root * (1.5 - 0.5 * block[m, m] * root * root)))
        out.append(jnp.where(lane < k + GROUP, jnp.concatenate(scaled, axis=0), 0.0))
    return out


def image_kernel(pressures, mine, other, y_ref, basis_ref, image_ref, held, arrived, inverse):
    arriving = fetch(pressures, held, arrived)
    first = own_core() == 0
    low = jnp.where(first, mine[...], other[...])
    high = jnp.where(first, other[...], mine[...])
    for i, rows in enumerate(inverse_factor(jnp.concatenate([low, high], axis=0))):
        inverse[GROUP * i : GROUP * (i + 1), :] = rows
    basis = lax.dot_general(
        y_ref[...],
        inverse[...],
        (((1,), (1,)), ((), ())),
        precision=lax.Precision.HIGHEST,
        preferred_element_type=F32,
    ).astype(BF16)
    basis_ref[...] = basis
    for copy, r in arriving:
        copy.wait()
        image_ref[r, :] = jnp.dot(held[r, :], basis, preferred_element_type=F32).astype(BF16)


def basis_and_image(pressures, mine, other, y_rows):
    panels = pressures.shape[0]
    samples, modes = y_rows.shape
    return pl.pallas_call(
        image_kernel,
        out_shape=(
            jax.ShapeDtypeStruct((samples, modes), BF16),
            jax.ShapeDtypeStruct((panels, modes), BF16),
        ),
        in_specs=[IN_HBM, IN_VMEM, IN_VMEM, IN_VMEM],
        out_specs=(IN_VMEM, IN_VMEM),
        scratch_shapes=[*held_like(pressures), pltpu.VMEM((modes, modes), F32)],
        compiler_params=ROOM,
    )(pressures, mine, other, y_rows)


def swap_cores(x):
    return lax.ppermute(x, "panel", [(i, i ^ 1) for i in range(lax.axis_size("panel"))])


def exchange(x, axis, groups=None):
    return lax.all_to_all(x, axis, 0, 0, axis_index_groups=groups)


def on_device(pressures, sketch):
    pressures = pltpu.with_memory_space_constraint(pressures, pltpu.HBM)
    panels, samples = pressures.shape
    modes = sketch.shape[1]
    blocks = lax.axis_size("tm")
    chips = lax.axis_size("panel") // 2
    same_core = [[2 * z + c for z in range(chips)] for c in range(2)]

    gathered = exchange(jnp.broadcast_to(sketch[None], (blocks, *sketch.shape)), "tm")
    keep, give = projection(pressures, gathered.reshape(panels, modes), chips)
    own = jnp.sum(exchange(keep + swap_cores(give), "panel", same_core), axis=0)
    mine = exchange(jnp.broadcast_to(own[None], (chips, *own.shape)), "panel", same_core)
    y_rows, half = rows_and_gram(mine, swap_cores(mine), blocks)
    half = jnp.sum(exchange(half, "tm"), axis=0)
    basis_rows, partial_image = basis_and_image(
        pressures, half, swap_cores(half), y_rows.reshape(samples, modes)
    )
    image = jnp.sum(exchange(partial_image.reshape(blocks, -1, modes), "tm").astype(F32), axis=0)
    return (basis_rows, image)


def solution(mesh):
    return jax.shard_map(
        on_device,
        mesh=mesh,
        in_specs=(P("panel", "tm"), P(("panel", "tm"), None)),
        out_specs=(P("tm", None), P(("panel", "tm"), None)),
        check_vma=False,
    )
```

time: 132 us -> 124 us (0.939)
  waiting for transfers between devices: 14.9 us -> 4.06 us
  blocking collectives: 93.4 us -> 101 us
  starting transfers between devices: 3.9 us -> 0.19 us
    all_to_all x1 -> x0, waiting for transfers between devices: 13.7 us -> none  [spread(): lax.all_to_all(jnp.broadcast_to(block[None], (size, *block.shape)), axis,...]
    all_to_all x4 -> x5, blocking collectives: 93.4 us -> 101 us  [exchange(): return lax.all_to_all(x, axis, 0, 0, axis_index_groups=groups)]
    all_to_all x1 -> x0, starting transfers between devices: 3.72 us -> none  [spread(): lax.all_to_all(jnp.broadcast_to(block[None], (size, *block.shape)), axis,...]
    ppermute x1 -> x3, waiting for transfers between devices: 1.11 us -> 4.06 us  [swap_cores(): lax.ppermute(x, 'panel', [(i, i ^ 1) for i in range(lax.axis_size('panel'...]
    pallas_call x1 -> x2, Pallas kernels: 4.32 us -> 4.89 us  [the longest x1 4.32 us: projection(): pl.pallas_call(projection_kernel, out_shape=(half, half), in_specs=[IN_HB...]
  transfers between devices with their start and end apart: 2 -> 3, of which waited for: 2 -> 3; matrix products, arithmetic and copies ran while one was open for 0% -> 0% of each run, Pallas kernels for 0% -> 0%
where the time goes in v3:
time: 124 us; the launch traced here: 123 us
  blocking collectives  101 us (81%)
  Pallas kernels  14.6 us (12%)
  waiting for transfers between devices  4.06 us (3%)
    all_to_all x5, blocking collectives, exchange(): return lax.all_to_all(x, axis, 0, 0, axis_index_groups=groups)  101 us
    pallas_call x1, Pallas kernels, basis_and_image(): pl.pallas_call(image_kernel, out_shape=(jax.ShapeDtypeStruct((samples, mo...  9.67 us
    pallas_call x1, Pallas kernels, projection(): pl.pallas_call(projection_kernel, out_shape=(half, half), in_specs=[IN_HB...  4.32 us
    ppermute x3, waiting for transfers between devices, swap_cores(): lax.ppermute(x, 'panel', [(i, i ^ 1) for i in range(lax.axis_size('panel'...  4.06 us
  transfers between devices with their start and end apart: 3, of which 3 were waited for; matrix products, arithmetic and copies ran while one was open for 0% of the time, Pallas kernels for 0%

profile of v3, /device:TPU:8, one launch (start us, length us, event | category | flops | bytes accessed | tf_op | source)
XLA Modules:
  0.0 123.0 jit_solution(16353003322561238550)
XLA Ops:
  0.6 1.2 broadcast_in_dim.4
  1.8 28.2 %all_to_all.25 = bf16[16,384,128]{2,1,0:T(8,128)(2,1)S(1)} all-to-all(bf16[16,384,128]{2,1,0:T(8,128)(2,1)S(1)} %broadcast_in_dim.4), channel_id=1, replica_groups=mesh['panel'=16,'tm'=16] {'tm'}, dimensions={0} | all-to-all | bytes 3145728 | tf_op jit(solution)/shard_map/all_to_all | solution.py:183
  30.0 4.3 %shard_map.41 = (f32[8,48,128]{2,1,0:T(8,128)S(1)}, f32[8,48,128]{2,1,0:T(8,128)S(1)}) custom-call(bf16[6144,768]{1,0:T(8,128)(2,1)} %pressures.3, bf16[6144,128]{1,0:T(8,128)(2,1)S(1)} %bitcast.3), custom_call_target="tpu_custom_call" | custom-call | tf_op jit(solution)/shard_map/pallas_call | solution.py:51
  34.4 0.1 collective-permute-start
  34.5 1.4 %collective-permute-done = f32[8,48,128]{2,1,0:T(8,128)S(1)} collective-permute-done((f32[8,48,128]{2,1,0:T(8,128)S(1)}, f32[8,48,128]{2,1,0:T(8,128)S(1)}, u32[]{:S(2)}, u32[]{:S(2)}) %collective-permute-start) | collective-permute-done | bytes 196640 | tf_op jit(solution)/shard_map/ppermute | solution.py:179
  35.9 19.0 %all_to_all.26 = f32[8,48,128]{2,1,0:T(8,128)S(1)} all-to-all(f32[8,48,128]{2,1,0:T(8,128)S(1)} %add.3), channel_id=1, replica_groups={{0,32,64,96,128,160,192,224},{16,48,80,112,144,176,208,240},{1,33,65,97..., dimensions={0} | all-to-all | bytes 393216 | tf_op jit(solution)/shard_map/all_to_all | solution.py:183
  55.0 12.2 %all_to_all.27.mine = f32[8,48,128]{2,1,0:T(8,128)S(1)} all-to-all(f32[8,48,128]{2,1,0:T(8,128)S(1)} %broadcast_in_dim.5), channel_id=1, replica_groups={{0,32,64,96,128,160,192,224},{16,48,80,112,144,176,208,240},{1,33,65,97..., dimensions={0} | all-to-all | bytes 393216 | tf_op jit(solution)/shard_map/all_to_all | solution.py:183
  67.2 0.0 collective-permute-start.1
  67.2 1.4 %collective-permute-done.1.other = f32[8,48,128]{2,1,0:T(8,128)S(1)} collective-permute-done((f32[8,48,128]{2,1,0:T(8,128)S(1)}, f32[8,48,128]{2,1,0:T(8,128)S(1)}, u32[]{:S(2)}, u32[]{:S(2)}) %collective-permute-start.1) | collective-permute-done | bytes 196640 | tf_op jit(solution)/shard_map/ppermute | solution.py:179
  68.6 0.6 shard_map.42
  69.2 15.6 %all_to_all.28 = f32[16,64,128]{2,1,0:T(8,128)S(1)} all-to-all(f32[16,64,128]{2,1,0:T(8,128)S(1)} %get-tuple-element.10), channel_id=1, replica_groups=mesh['panel'=16,'tm'=16] {'tm'}, dimensions={0} | all-to-all | bytes 1048576 | tf_op jit(solution)/shard_map/all_to_all | solution.py:183
  84.8 0.1 collective-permute-start.2
  84.9 1.2 collective-permute-done.2.other
  86.1 9.7 %shard_map.43 = (bf16[768,128]{1,0:T(8,128)(2,1)}, bf16[6144,128]{1,0:T(8,128)(2,1)S(1)}) custom-call(bf16[6144,768]{1,0:T(8,128)(2,1)} %pressures.3, f32[64,128]{1,0:T(8,128)S(1)} %reduce_sum.28.mine, f32[64,128]{1,0:T(8,128)S(1)} %collective-permute-done.2.other, f32[768,128]{1,0:T(8,128)S(1)} %bitcast.5), custom_call_target="tpu_custom_call" | custom-call | tf_op jit(solution)/shard_map/pallas_call | solution.py:165
  95.8 26.3 %all_to_all.29 = bf16[16,384,128]{2,1,0:T(8,128)(2,1)S(1)} all-to-all(bf16[16,384,128]{2,1,0:T(8,128)(2,1)S(1)} %bitcast.4), channel_id=1, replica_groups=mesh['panel'=16,'tm'=16] {'tm'}, dimensions={0} | all-to-all | bytes 3145728 | tf_op jit(solution)/shard_map/all_to_all | solution.py:183
  122.1 0.9 convert_reduce_fusion
  (4 shorter events, 0.1 us)
Async XLA Ops:
  34.4 1.5 %collective-permute-start = (f32[8,48,128]{2,1,0:T(8,128)S(1)}, f32[8,48,128]{2,1,0:T(8,128)S(1)}, u32[]{:S(2)}, u32[]{:S(2)}) collective-permute-start(f32[8,48,128]{2,1,0:T(8,128)S(1)} %get-tuple-element.9), channel_id=1, source_target_pairs={{0,16},{16,0},{32,48},{48,32},{64,80},{80,64},{96,112},{112,96},{1... | collective-permute-start | bytes 589832 | tf_op jit(solution)/shard_map/ppermute | solution.py:179
  67.2 1.4 %collective-permute-start.1 = (f32[8,48,128]{2,1,0:T(8,128)S(1)}, f32[8,48,128]{2,1,0:T(8,128)S(1)}, u32[]{:S(2)}, u32[]{:S(2)}) collective-permute-start(f32[8,48,128]{2,1,0:T(8,128)S(1)} %all_to_all.27.mine), channel_id=1, source_target_pairs={{0,16},{16,0},{32,48},{48,32},{64,80},{80,64},{96,112},{112,96},{1... | collective-permute-start | bytes 589832 | tf_op jit(solution)/shard_map/ppermute | solution.py:179
  84.8 1.3 %collective-permute-start.2 = (f32[64,128]{1,0:T(8,128)S(1)}, f32[64,128]{1,0:T(8,128)S(1)}, u32[]{:S(2)}, u32[]{:S(2)}) collective-permute-start(f32[64,128]{1,0:T(8,128)S(1)} %reduce_sum.28.mine), channel_id=1, source_target_pairs={{0,16},{16,0},{32,48},{48,32},{64,80},{80,64},{96,112},{112,96},{1... | collective-permute-start | bytes 98312 | tf_op jit(solution)/shard_map/ppermute | solution.py:179

commit v4 on v3

--- a/solution.py
+++ b/solution.py
@@ -1,3 +1,5 @@
+import math
+
 import jax
 import jax.numpy as jnp
 from jax import lax
@@ -58,16 +60,15 @@
     )(pressures, sketch)
 
 
-def gram_kernel(mine, other, y_ref, half_ref):
+def gram_kernel(mine, other, y_ref, copies_ref):
     first = own_core() == 0
     y_ref[:, 0] = jnp.where(first, mine[...], other[...])
     y_ref[:, 1] = jnp.where(first, other[...], mine[...])
-    copies, half, modes = half_ref.shape
-    y = y_ref[...].reshape(-1, modes)
+    y = y_ref[...].reshape(-1, y_ref.shape[3])
     gram = lax.dot_general(
         y, y, (((0,), (0,)), ((), ())), precision=lax.Precision.HIGHEST, preferred_element_type=F32
     )
-    half_ref[...] = jnp.broadcast_to(jnp.where(first, gram[:half], gram[half:])[None], half_ref.shape)
+    copies_ref[...] = jnp.broadcast_to(gram[None], copies_ref.shape)
 
 
 def rows_and_gram(mine, other, copies):
@@ -76,7 +77,7 @@
         gram_kernel,
         out_shape=(
             jax.ShapeDtypeStruct((chips, 2, rows, modes), F32),
-            jax.ShapeDtypeStruct((copies, modes // 2, modes), F32),
+            jax.ShapeDtypeStruct((copies, modes, modes), F32),
         ),
         in_specs=[IN_VMEM, IN_VMEM],
         out_specs=(IN_VMEM, IN_VMEM),
@@ -139,12 +140,9 @@
     return out
 
 
-def image_kernel(pressures, mine, other, y_ref, basis_ref, image_ref, held, arrived, inverse):
+def image_kernel(pressures, gram_parts, y_ref, basis_ref, image_ref, held, arrived, inverse):
     arriving = fetch(pressures, held, arrived)
-    first = own_core() == 0
-    low = jnp.where(first, mine[...], other[...])
-    high = jnp.where(first, other[...], mine[...])
-    for i, rows in enumerate(inverse_factor(jnp.concatenate([low, high], axis=0))):
+    for i, rows in enumerate(inverse_factor(jnp.sum(gram_parts[...], axis=0))):
         inverse[GROUP * i : GROUP * (i + 1), :] = rows
     basis = lax.dot_general(
         y_ref[...],
@@ -159,7 +157,7 @@
         image_ref[r, :] = jnp.dot(held[r, :], basis, preferred_element_type=F32).astype(BF16)
 
 
-def basis_and_image(pressures, mine, other, y_rows):
+def basis_and_image(pressures, gram_parts, y_rows):
     panels = pressures.shape[0]
     samples, modes = y_rows.shape
     return pl.pallas_call(
@@ -168,11 +166,11 @@
             jax.ShapeDtypeStruct((samples, modes), BF16),
             jax.ShapeDtypeStruct((panels, modes), BF16),
         ),
-        in_specs=[IN_HBM, IN_VMEM, IN_VMEM, IN_VMEM],
+        in_specs=[IN_HBM, IN_VMEM, IN_VMEM],
         out_specs=(IN_VMEM, IN_VMEM),
         scratch_shapes=[*held_like(pressures), pltpu.VMEM((modes, modes), F32)],
         compiler_params=ROOM,
-    )(pressures, mine, other, y_rows)
+    )(pressures, gram_parts, y_rows)
 
 
 def swap_cores(x):
@@ -189,17 +187,19 @@
     modes = sketch.shape[1]
     blocks = lax.axis_size("tm")
     chips = lax.axis_size("panel") // 2
+    side = math.isqrt(blocks)
+    same_x = [[x * side + y for y in range(side)] for x in range(side)]
+    same_y = [[x * side + y for x in range(side)] for y in range(side)]
     same_core = [[2 * z + c for z in range(chips)] for c in range(2)]
 
     gathered = exchange(jnp.broadcast_to(sketch[None], (blocks, *sketch.shape)), "tm")
     keep, give = projection(pressures, gathered.reshape(panels, modes), chips)
     own = jnp.sum(exchange(keep + swap_cores(give), "panel", same_core), axis=0)
     mine = exchange(jnp.broadcast_to(own[None], (chips, *own.shape)), "panel", same_core)
-    y_rows, half = rows_and_gram(mine, swap_cores(mine), blocks)
-    half = jnp.sum(exchange(half, "tm"), axis=0)
-    basis_rows, partial_image = basis_and_image(
-        pressures, half, swap_cores(half), y_rows.reshape(samples, modes)
-    )
+    y_rows, gram = rows_and_gram(mine, swap_cores(mine), side)
+    line = jnp.sum(exchange(gram, "tm", same_x), axis=0)
+    gram_parts = exchange(jnp.broadcast_to(line[None], gram.shape), "tm", same_y)
+    basis_rows, partial_image = basis_and_image(pressures, gram_parts, y_rows.reshape(samples, modes))
     image = jnp.sum(exchange(partial_image.reshape(blocks, -1, modes), "tm").astype(F32), axis=0)
     return (basis_rows, image)
 

time: 124 us -> 123 us (level)
    ppermute x3 -> x2, waiting for transfers between devices: 4.06 us -> 2.87 us  [swap_cores(): lax.ppermute(x, 'panel', [(i, i ^ 1) for i in range(lax.axis_size('panel'...]
    all_to_all x5 -> x6, blocking collectives: 101 us -> 102 us  [exchange(): return lax.all_to_all(x, axis, 0, 0, axis_index_groups=groups)]
  transfers between devices with their start and end apart: 3 -> 2, of which waited for: 3 -> 2; matrix products, arithmetic and copies ran while one was open for 0% -> 0% of each run, Pallas kernels for 0% -> 0%
where the time goes in v4:
time: 123 us
  blocking collectives  102 us (83%)
  Pallas kernels  14.6 us (12%)
  waiting for transfers between devices  2.87 us (2%)
    all_to_all x6, blocking collectives, exchange(): return lax.all_to_all(x, axis, 0, 0, axis_index_groups=groups)  102 us
    pallas_call x1, Pallas kernels, basis_and_image(): pl.pallas_call(image_kernel, out_shape=(jax.ShapeDtypeStruct((samples, mo...  9.75 us
    pallas_call x1, Pallas kernels, projection(): pl.pallas_call(projection_kernel, out_shape=(half, half), in_specs=[IN_HB...  4.32 us
    ppermute x2, waiting for transfers between devices, swap_cores(): lax.ppermute(x, 'panel', [(i, i ^ 1) for i in range(lax.axis_size('panel'...  2.87 us
  transfers between devices with their start and end apart: 2, of which 2 were waited for; matrix products, arithmetic and copies ran while one was open for 0% of the time, Pallas kernels for 0%

profile of v4, /device:TPU:8, one launch (start us, length us, event | category | flops | bytes accessed | tf_op | source)
XLA Modules:
  0.0 122.6 jit_solution(1207277124100447177)
XLA Ops:
  0.6 1.2 broadcast_in_dim.6
  1.8 28.2 %all_to_all.30 = bf16[16,384,128]{2,1,0:T(8,128)(2,1)S(1)} all-to-all(bf16[16,384,128]{2,1,0:T(8,128)(2,1)S(1)} %broadcast_in_dim.6), channel_id=1, replica_groups=mesh['panel'=16,'tm'=16] {'tm'}, dimensions={0} | all-to-all | bytes 3145728 | tf_op jit(solution)/shard_map/all_to_all | solution.py:181
  30.0 4.3 %shard_map.41 = (f32[8,48,128]{2,1,0:T(8,128)S(1)}, f32[8,48,128]{2,1,0:T(8,128)S(1)}) custom-call(bf16[6144,768]{1,0:T(8,128)(2,1)} %pressures.3, bf16[6144,128]{1,0:T(8,128)(2,1)S(1)} %bitcast.3), custom_call_target="tpu_custom_call" | custom-call | tf_op jit(solution)/shard_map/pallas_call | solution.py:53
  34.4 0.1 collective-permute-start
  34.5 1.4 %collective-permute-done = f32[8,48,128]{2,1,0:T(8,128)S(1)} collective-permute-done((f32[8,48,128]{2,1,0:T(8,128)S(1)}, f32[8,48,128]{2,1,0:T(8,128)S(1)}, u32[]{:S(2)}, u32[]{:S(2)}) %collective-permute-start) | collective-permute-done | bytes 196640 | tf_op jit(solution)/shard_map/ppermute | solution.py:177
  35.9 19.0 %all_to_all.31 = f32[8,48,128]{2,1,0:T(8,128)S(1)} all-to-all(f32[8,48,128]{2,1,0:T(8,128)S(1)} %add.3), channel_id=1, replica_groups={{0,32,64,96,128,160,192,224},{16,48,80,112,144,176,208,240},{1,33,65,97..., dimensions={0} | all-to-all | bytes 393216 | tf_op jit(solution)/shard_map/all_to_all | solution.py:181
  55.0 12.2 %all_to_all.32.mine = f32[8,48,128]{2,1,0:T(8,128)S(1)} all-to-all(f32[8,48,128]{2,1,0:T(8,128)S(1)} %broadcast_in_dim.7), channel_id=1, replica_groups={{0,32,64,96,128,160,192,224},{16,48,80,112,144,176,208,240},{1,33,65,97..., dimensions={0} | all-to-all | bytes 393216 | tf_op jit(solution)/shard_map/all_to_all | solution.py:181
  67.2 0.0 collective-permute-start.1
  67.2 1.4 %collective-permute-done.1.other = f32[8,48,128]{2,1,0:T(8,128)S(1)} collective-permute-done((f32[8,48,128]{2,1,0:T(8,128)S(1)}, f32[8,48,128]{2,1,0:T(8,128)S(1)}, u32[]{:S(2)}, u32[]{:S(2)}) %collective-permute-start.1) | collective-permute-done | bytes 196640 | tf_op jit(solution)/shard_map/ppermute | solution.py:177
  68.6 0.5 shard_map.42
  69.1 9.8 %all_to_all.33 = f32[4,128,128]{2,1,0:T(8,128)S(1)} all-to-all(f32[4,128,128]{2,1,0:T(8,128)S(1)} %get-tuple-element.10), channel_id=1, replica_groups={{0,1,2,3},{4,5,6,7},{8,9,10,11},{12,13,14,15},{16,17,18,19},{20,21,22,2..., dimensions={0} | all-to-all | bytes 524288 | tf_op jit(solution)/shard_map/all_to_all | solution.py:181
  79.0 9.2 %all_to_all.34.gram_parts = f32[4,128,128]{2,1,0:T(8,128)S(1)} all-to-all(f32[4,128,128]{2,1,0:T(8,128)S(1)} %broadcast_in_dim.8), channel_id=1, replica_groups={{0,4,8,12},{1,5,9,13},{2,6,10,14},{3,7,11,15},{16,20,24,28},{17,21,25,2..., dimensions={0} | all-to-all | bytes 524288 | tf_op jit(solution)/shard_map/all_to_all | solution.py:181
  88.2 9.7 %shard_map.43 = (bf16[768,128]{1,0:T(8,128)(2,1)}, bf16[6144,128]{1,0:T(8,128)(2,1)S(1)}) custom-call(bf16[6144,768]{1,0:T(8,128)(2,1)} %pressures.3, f32[4,128,128]{2,1,0:T(8,128)S(1)} %all_to_all.34.gram_parts, f32[768,128]{1,0:T(8,128)S(1)} %bitcast.5), custom_call_target="tpu_custom_call" | custom-call | tf_op jit(solution)/shard_map/pallas_call | solution.py:163
  98.0 23.8 %all_to_all.35 = bf16[16,384,128]{2,1,0:T(8,128)(2,1)S(1)} all-to-all(bf16[16,384,128]{2,1,0:T(8,128)(2,1)S(1)} %bitcast.4), channel_id=1, replica_groups=mesh['panel'=16,'tm'=16] {'tm'}, dimensions={0} | all-to-all | bytes 3145728 | tf_op jit(solution)/shard_map/all_to_all | solution.py:181
  121.7 0.9 convert_reduce_fusion
  (5 shorter events, 0.1 us)
Async XLA Ops:
  34.4 1.5 %collective-permute-start = (f32[8,48,128]{2,1,0:T(8,128)S(1)}, f32[8,48,128]{2,1,0:T(8,128)S(1)}, u32[]{:S(2)}, u32[]{:S(2)}) collective-permute-start(f32[8,48,128]{2,1,0:T(8,128)S(1)} %get-tuple-element.9), channel_id=1, source_target_pairs={{0,16},{16,0},{32,48},{48,32},{64,80},{80,64},{96,112},{112,96},{1... | collective-permute-start | bytes 589832 | tf_op jit(solution)/shard_map/ppermute | solution.py:177
  67.2 1.4 %collective-permute-start.1 = (f32[8,48,128]{2,1,0:T(8,128)S(1)}, f32[8,48,128]{2,1,0:T(8,128)S(1)}, u32[]{:S(2)}, u32[]{:S(2)}) collective-permute-start(f32[8,48,128]{2,1,0:T(8,128)S(1)} %all_to_all.32.mine), channel_id=1, source_target_pairs={{0,16},{16,0},{32,48},{48,32},{64,80},{80,64},{96,112},{112,96},{1... | collective-permute-start | bytes 589832 | tf_op jit(solution)/shard_map/ppermute | solution.py:177

commit v5 on v4

--- a/solution.py
+++ b/solution.py
@@ -1,3 +1,4 @@
+import functools
 import math
 
 import jax
@@ -16,46 +17,55 @@
 ROOM = pltpu.CompilerParams(vmem_limit_bytes=32 << 20)
 
 
-def fetch(pressures, held, arrived):
-    rows = held.shape[0] // PIECES
-    parts = [pl.ds(i * rows, rows) for i in range(PIECES)]
-    copies = [pltpu.make_async_copy(pressures.at[r], held.at[r], arrived.at[i]) for i, r in enumerate(parts)]
+def own_core():
+    return lax.rem(lax.axis_index("panel"), 2)
+
+
+def fetch(pressures, held, arrived, sources):
+    rows = held.shape[0] // len(sources)
+    copies, parts = [], []
+    for i, source in enumerate(sources):
+        start = source * rows if isinstance(source, int) else pl.multiple_of(source * rows, rows)
+        parts.append(pl.ds(i * rows, rows))
+        copies.append(pltpu.make_async_copy(pressures.at[pl.ds(start, rows)], held.at[parts[-1]], arrived.at[i]))
     for copy in copies:
         copy.start()
     return list(zip(copies, parts))
 
 
-def held_like(pressures):
-    return [pltpu.VMEM(pressures.shape, pressures.dtype), pltpu.SemaphoreType.DMA((PIECES,))]
-
-
-def own_core():
-    return lax.rem(lax.axis_index("panel"), 2)
-
-
-def projection_kernel(pressures, sketch, keep_ref, give_ref, held, arrived):
+def held_like(pressures, pieces):
+    return [pltpu.VMEM(pressures.shape, pressures.dtype), pltpu.SemaphoreType.DMA((pieces,))]
+
+
+def projection_kernel(side, pressures, sketch, keep_ref, give_ref, held, arrived):
+    first = own_core() == 0
+    blocks = [(a, b) for a in range(side) for b in range(side)]
+    sources = [jnp.where(first, a * side + b, b * side + a) for a, b in blocks]
+    arriving = fetch(pressures, held, arrived, sources)
     total = None
-    for copy, r in fetch(pressures, held, arrived):
-        copy.wait()
+    for i in range(0, len(arriving), side):
+        for copy, _ in arriving[i : i + side]:
+            copy.wait()
+        rows = side * (held.shape[0] // len(blocks))
+        r = pl.ds((i // side) * rows, rows)
         term = lax.dot_general(sketch[r, :], held[r, :], (((0,), (0,)), ((), ())), preferred_element_type=F32)
         total = term if total is None else total + term
     chips, rows, modes = keep_ref.shape
     y = total.T.reshape(chips, 2, rows, modes)
-    first = own_core() == 0
     keep_ref[...] = jnp.where(first, y[:, 0], y[:, 1])
     give_ref[...] = jnp.where(first, y[:, 1], y[:, 0])
 
 
-def projection(pressures, sketch, chips):
+def projection(pressures, sketch, chips, side):
     samples = pressures.shape[1]
     modes = sketch.shape[1]
     half = jax.ShapeDtypeStruct((chips, samples // (2 * chips), modes), F32)
     return pl.pallas_call(
-        projection_kernel,
+        functools.partial(projection_kernel, side),
         out_shape=(half, half),
         in_specs=[IN_HBM, IN_VMEM],
         out_specs=(IN_VMEM, IN_VMEM),
-        scratch_shapes=held_like(pressures),
+        scratch_shapes=held_like(pressures, side * side),
         compiler_params=ROOM,
     )(pressures, sketch)
 
@@ -141,7 +151,7 @@
 
 
 def image_kernel(pressures, gram_parts, y_ref, basis_ref, image_ref, held, arrived, inverse):
-    arriving = fetch(pressures, held, arrived)
+    arriving = fetch(pressures, held, arrived, range(PIECES))
     for i, rows in enumerate(inverse_factor(jnp.sum(gram_parts[...], axis=0))):
         inverse[GROUP * i : GROUP * (i + 1), :] = rows
     basis = lax.dot_general(
@@ -168,7 +178,7 @@
         ),
         in_specs=[IN_HBM, IN_VMEM, IN_VMEM],
         out_specs=(IN_VMEM, IN_VMEM),
-        scratch_shapes=[*held_like(pressures), pltpu.VMEM((modes, modes), F32)],
+        scratch_shapes=[*held_like(pressures, PIECES), pltpu.VMEM((modes, modes), F32)],
         compiler_params=ROOM,
     )(pressures, gram_parts, y_rows)
 
@@ -179,6 +189,20 @@
 
 def exchange(x, axis, groups=None):
     return lax.all_to_all(x, axis, 0, 0, axis_index_groups=groups)
+
+
+def turns(across, side):
+    along = [[], []]
+    for p in range(across):
+        at = [[p * side * side + x * side + y for y in range(side)] for x in range(side)]
+        lines = [at, [list(column) for column in zip(*at)]]
+        for turn in range(2):
+            along[turn] += lines[(p + turn) % 2]
+    return along
+
+
+def copies_of(x, count):
+    return jnp.broadcast_to(x[None], (count, *x.shape))
 
 
 def on_device(pressures, sketch):
@@ -186,19 +210,22 @@
     panels, samples = pressures.shape
     modes = sketch.shape[1]
     blocks = lax.axis_size("tm")
-    chips = lax.axis_size("panel") // 2
+    across = lax.axis_size("panel")
+    chips = across // 2
     side = math.isqrt(blocks)
     same_x = [[x * side + y for y in range(side)] for x in range(side)]
     same_y = [[x * side + y for x in range(side)] for y in range(side)]
     same_core = [[2 * z + c for z in range(chips)] for c in range(2)]
-
-    gathered = exchange(jnp.broadcast_to(sketch[None], (blocks, *sketch.shape)), "tm")
-    keep, give = projection(pressures, gathered.reshape(panels, modes), chips)
+    one_way, other_way = turns(across, side)
+
+    line = exchange(copies_of(sketch, side), ("panel", "tm"), one_way)
+    gathered = exchange(copies_of(line, side), ("panel", "tm"), other_way)
+    keep, give = projection(pressures, gathered.reshape(panels, modes), chips, side)
     own = jnp.sum(exchange(keep + swap_cores(give), "panel", same_core), axis=0)
-    mine = exchange(jnp.broadcast_to(own[None], (chips, *own.shape)), "panel", same_core)
+    mine = exchange(copies_of(own, chips), "panel", same_core)
     y_rows, gram = rows_and_gram(mine, swap_cores(mine), side)
     line = jnp.sum(exchange(gram, "tm", same_x), axis=0)
-    gram_parts = exchange(jnp.broadcast_to(line[None], gram.shape), "tm", same_y)
+    gram_parts = exchange(copies_of(line, side), "tm", same_y)
     basis_rows, partial_image = basis_and_image(pressures, gram_parts, y_rows.reshape(samples, modes))
     image = jnp.sum(exchange(partial_image.reshape(blocks, -1, modes), "tm").astype(F32), axis=0)
     return (basis_rows, image)

time: 123 us -> 123 us (level)
    all_to_all x6 -> x7, blocking collectives: 102 us -> 102 us  [exchange(): return lax.all_to_all(x, axis, 0, 0, axis_index_groups=groups)]
where the time goes in v5:
time: 123 us
  blocking collectives  102 us (83%)
  Pallas kernels  14.8 us (12%)
  waiting for transfers between devices  2.87 us (2%)
  local copies, waits for them, and re-layouts  1.28 us (1%)
    all_to_all x7, blocking collectives, exchange(): return lax.all_to_all(x, axis, 0, 0, axis_index_groups=groups)  102 us
    pallas_call x1, Pallas kernels, basis_and_image(): pl.pallas_call(image_kernel, out_shape=(jax.ShapeDtypeStruct((samples, mo...  9.74 us
    pallas_call x1, Pallas kernels, projection(): pl.pallas_call(functools.partial(projection_kernel, side), out_shape=(hal...  4.51 us
    ppermute x2, waiting for transfers between devices, swap_cores(): lax.ppermute(x, 'panel', [(i, i ^ 1) for i in range(lax.axis_size('panel'...  2.87 us
  transfers between devices with their start and end apart: 2, of which 2 were waited for; matrix products, arithmetic and copies ran while one was open for 0% of the time, Pallas kernels for 0%

profile of v5, /device:TPU:8, one launch (start us, length us, event | category | flops | bytes accessed | tf_op | source)
XLA Modules:
  0.0 123.1 jit_solution(954388069716299552)
XLA Ops:
  0.6 0.9 broadcast_in_dim.8
  1.6 10.6 %all_to_all.35 = bf16[4,384,128]{2,1,0:T(8,128)(2,1)S(1)} all-to-all(bf16[4,384,128]{2,1,0:T(8,128)(2,1)S(1)} %broadcast_in_dim.8), channel_id=1, replica_groups={{0,1,2,3},{4,5,6,7},{8,9,10,11},{12,13,14,15},{16,20,24,28},{17,21,25,2..., dimensions={0} | all-to-all | bytes 786432 | tf_op jit(solution)/shard_map/all_to_all | solution.py:191
  12.2 0.3 broadcast_in_dim.9
  12.5 17.8 %all_to_all.36 = bf16[4,4,384,128]{3,2,1,0:T(8,128)(2,1)S(1)} all-to-all(bf16[4,4,384,128]{3,2,1,0:T(8,128)(2,1)S(1)} %broadcast_in_dim.9), channel_id=1, replica_groups={{0,4,8,12},{1,5,9,13},{2,6,10,14},{3,7,11,15},{16,17,18,19},{20,21,22,2..., dimensions={0} | all-to-all | bytes 3145728 | tf_op jit(solution)/shard_map/all_to_all | solution.py:191
  30.3 4.5 %shard_map.41 = (f32[8,48,128]{2,1,0:T(8,128)S(1)}, f32[8,48,128]{2,1,0:T(8,128)S(1)}) custom-call(bf16[6144,768]{1,0:T(8,128)(2,1)} %pressures.3, bf16[6144,128]{1,0:T(8,128)(2,1)S(1)} %bitcast.3), custom_call_target="tpu_custom_call" | custom-call | tf_op jit(solution)/shard_map/pallas_call | solution.py:63
  34.8 0.1 collective-permute-start
  34.9 1.4 %collective-permute-done = f32[8,48,128]{2,1,0:T(8,128)S(1)} collective-permute-done((f32[8,48,128]{2,1,0:T(8,128)S(1)}, f32[8,48,128]{2,1,0:T(8,128)S(1)}, u32[]{:S(2)}, u32[]{:S(2)}) %collective-permute-start) | collective-permute-done | bytes 196640 | tf_op jit(solution)/shard_map/ppermute | solution.py:187
  36.4 19.0 %all_to_all.37 = f32[8,48,128]{2,1,0:T(8,128)S(1)} all-to-all(f32[8,48,128]{2,1,0:T(8,128)S(1)} %add.3), channel_id=1, replica_groups={{0,32,64,96,128,160,192,224},{16,48,80,112,144,176,208,240},{1,33,65,97..., dimensions={0} | all-to-all | bytes 393216 | tf_op jit(solution)/shard_map/all_to_all | solution.py:191
  55.5 12.2 %all_to_all.38.mine = f32[8,48,128]{2,1,0:T(8,128)S(1)} all-to-all(f32[8,48,128]{2,1,0:T(8,128)S(1)} %broadcast_in_dim.10), channel_id=1, replica_groups={{0,32,64,96,128,160,192,224},{16,48,80,112,144,176,208,240},{1,33,65,97..., dimensions={0} | all-to-all | bytes 393216 | tf_op jit(solution)/shard_map/all_to_all | solution.py:191
  67.7 0.0 collective-permute-start.1
  67.7 1.4 %collective-permute-done.1.other = f32[8,48,128]{2,1,0:T(8,128)S(1)} collective-permute-done((f32[8,48,128]{2,1,0:T(8,128)S(1)}, f32[8,48,128]{2,1,0:T(8,128)S(1)}, u32[]{:S(2)}, u32[]{:S(2)}) %collective-permute-start.1) | collective-permute-done | bytes 196640 | tf_op jit(solution)/shard_map/ppermute | solution.py:187
  69.1 0.5 shard_map.42
  69.6 9.6 %all_to_all.39 = f32[4,128,128]{2,1,0:T(8,128)S(1)} all-to-all(f32[4,128,128]{2,1,0:T(8,128)S(1)} %get-tuple-element.10), channel_id=1, replica_groups={{0,1,2,3},{4,5,6,7},{8,9,10,11},{12,13,14,15},{16,17,18,19},{20,21,22,2..., dimensions={0} | all-to-all | bytes 524288 | tf_op jit(solution)/shard_map/all_to_all | solution.py:191
  79.3 9.1 %all_to_all.40.gram_parts = f32[4,128,128]{2,1,0:T(8,128)S(1)} all-to-all(f32[4,128,128]{2,1,0:T(8,128)S(1)} %broadcast_in_dim.11), channel_id=1, replica_groups={{0,4,8,12},{1,5,9,13},{2,6,10,14},{3,7,11,15},{16,20,24,28},{17,21,25,2..., dimensions={0} | all-to-all | bytes 524288 | tf_op jit(solution)/shard_map/all_to_all | solution.py:191
  88.4 9.7 %shard_map.43 = (bf16[768,128]{1,0:T(8,128)(2,1)}, bf16[6144,128]{1,0:T(8,128)(2,1)S(1)}) custom-call(bf16[6144,768]{1,0:T(8,128)(2,1)} %pressures.3, f32[4,128,128]{2,1,0:T(8,128)S(1)} %all_to_all.40.gram_parts, f32[768,128]{1,0:T(8,128)S(1)} %bitcast.5), custom_call_target="tpu_custom_call" | custom-call | tf_op jit(solution)/shard_map/pallas_call | solution.py:173
  98.1 24.0 %all_to_all.41 = bf16[16,384,128]{2,1,0:T(8,128)(2,1)S(1)} all-to-all(bf16[16,384,128]{2,1,0:T(8,128)(2,1)S(1)} %bitcast.4), channel_id=1, replica_groups=mesh['panel'=16,'tm'=16] {'tm'}, dimensions={0} | all-to-all | bytes 3145728 | tf_op jit(solution)/shard_map/all_to_all | solution.py:191
  122.2 0.9 convert_reduce_fusion
  (5 shorter events, 0.1 us)
Async XLA Ops:
  34.8 1.5 %collective-permute-start = (f32[8,48,128]{2,1,0:T(8,128)S(1)}, f32[8,48,128]{2,1,0:T(8,128)S(1)}, u32[]{:S(2)}, u32[]{:S(2)}) collective-permute-start(f32[8,48,128]{2,1,0:T(8,128)S(1)} %get-tuple-element.9), channel_id=1, source_target_pairs={{0,16},{16,0},{32,48},{48,32},{64,80},{80,64},{96,112},{112,96},{1... | collective-permute-start | bytes 589832 | tf_op jit(solution)/shard_map/ppermute | solution.py:187
  67.7 1.4 %collective-permute-start.1 = (f32[8,48,128]{2,1,0:T(8,128)S(1)}, f32[8,48,128]{2,1,0:T(8,128)S(1)}, u32[]{:S(2)}, u32[]{:S(2)}) collective-permute-start(f32[8,48,128]{2,1,0:T(8,128)S(1)} %all_to_all.38.mine), channel_id=1, source_target_pairs={{0,16},{16,0},{32,48},{48,32},{64,80},{80,64},{96,112},{112,96},{1... | collective-permute-start | bytes 589832 | tf_op jit(solution)/shard_map/ppermute | solution.py:187

commit v6 on v3

--- a/solution.py
+++ b/solution.py
@@ -1,3 +1,5 @@
+import math
+
 import jax
 import jax.numpy as jnp
 from jax import lax
@@ -58,16 +60,16 @@
     )(pressures, sketch)
 
 
-def gram_kernel(mine, other, y_ref, half_ref):
+def gram_kernel(mine, other, y_ref, copies_ref):
     first = own_core() == 0
     y_ref[:, 0] = jnp.where(first, mine[...], other[...])
     y_ref[:, 1] = jnp.where(first, other[...], mine[...])
-    copies, half, modes = half_ref.shape
-    y = y_ref[...].reshape(-1, modes)
+    y = y_ref[...].reshape(-1, y_ref.shape[3])
     gram = lax.dot_general(
         y, y, (((0,), (0,)), ((), ())), precision=lax.Precision.HIGHEST, preferred_element_type=F32
     )
-    half_ref[...] = jnp.broadcast_to(jnp.where(first, gram[:half], gram[half:])[None], half_ref.shape)
+    half = copies_ref.shape[1]
+    copies_ref[...] = jnp.broadcast_to(jnp.where(first, gram[:half], gram[half:])[None], copies_ref.shape)
 
 
 def rows_and_gram(mine, other, copies):
@@ -183,20 +185,38 @@
     return lax.all_to_all(x, axis, 0, 0, axis_index_groups=groups)
 
 
+def turns(across, side):
+    along = [[], []]
+    for p in range(across):
+        at = [[p * side * side + x * side + y for y in range(side)] for x in range(side)]
+        lines = [at, [list(column) for column in zip(*at)]]
+        for turn in range(2):
+            along[turn] += lines[(p + turn) % 2]
+    return along
+
+
+def copies_of(x, count):
+    return jnp.broadcast_to(x[None], (count, *x.shape))
+
+
 def on_device(pressures, sketch):
     pressures = pltpu.with_memory_space_constraint(pressures, pltpu.HBM)
     panels, samples = pressures.shape
     modes = sketch.shape[1]
     blocks = lax.axis_size("tm")
-    chips = lax.axis_size("panel") // 2
+    across = lax.axis_size("panel")
+    chips = across // 2
+    side = math.isqrt(blocks)
     same_core = [[2 * z + c for z in range(chips)] for c in range(2)]
-
-    gathered = exchange(jnp.broadcast_to(sketch[None], (blocks, *sketch.shape)), "tm")
+    one_way, other_way = turns(across, side)
+
+    gathered = exchange(copies_of(sketch, blocks), "tm")
     keep, give = projection(pressures, gathered.reshape(panels, modes), chips)
     own = jnp.sum(exchange(keep + swap_cores(give), "panel", same_core), axis=0)
-    mine = exchange(jnp.broadcast_to(own[None], (chips, *own.shape)), "panel", same_core)
-    y_rows, half = rows_and_gram(mine, swap_cores(mine), blocks)
-    half = jnp.sum(exchange(half, "tm"), axis=0)
+    mine = exchange(copies_of(own, chips), "panel", same_core)
+    y_rows, half = rows_and_gram(mine, swap_cores(mine), side)
+    line = jnp.sum(exchange(half, ("panel", "tm"), one_way), axis=0)
+    half = jnp.sum(exchange(copies_of(line, side), ("panel", "tm"), other_way), axis=0)
     basis_rows, partial_image = basis_and_image(
         pressures, half, swap_cores(half), y_rows.reshape(samples, modes)
     )

time: 124 us -> 125 us (level)
  blocking collectives: 101 us -> 103 us
    all_to_all x5 -> x6, blocking collectives: 101 us -> 103 us  [exchange(): return lax.all_to_all(x, axis, 0, 0, axis_index_groups=groups)]
where the time goes in v6:
time: 125 us; the launch traced here: 124 us
  blocking collectives  103 us (82%)
  Pallas kernels  14.5 us (12%)
  waiting for transfers between devices  4.06 us (3%)
    all_to_all x6, blocking collectives, exchange(): return lax.all_to_all(x, axis, 0, 0, axis_index_groups=groups)  103 us
    pallas_call x1, Pallas kernels, basis_and_image(): pl.pallas_call(image_kernel, out_shape=(jax.ShapeDtypeStruct((samples, mo...  9.67 us
    pallas_call x1, Pallas kernels, projection(): pl.pallas_call(projection_kernel, out_shape=(half, half), in_specs=[IN_HB...  4.32 us
    ppermute x3, waiting for transfers between devices, swap_cores(): lax.ppermute(x, 'panel', [(i, i ^ 1) for i in range(lax.axis_size('panel'...  4.06 us
  transfers between devices with their start and end apart: 3, of which 3 were waited for; matrix products, arithmetic and copies ran while one was open for 0% of the time, Pallas kernels for 0%

profile of v6, /device:TPU:8, one launch (start us, length us, event | category | flops | bytes accessed | tf_op | source)
XLA Modules:
  0.0 124.4 jit_solution(1788785160482245255)
XLA Ops:
  0.6 1.2 broadcast_in_dim.6
  1.8 28.2 %all_to_all.30 = bf16[16,384,128]{2,1,0:T(8,128)(2,1)S(1)} all-to-all(bf16[16,384,128]{2,1,0:T(8,128)(2,1)S(1)} %broadcast_in_dim.6), channel_id=1, replica_groups=mesh['panel'=16,'tm'=16] {'tm'}, dimensions={0} | all-to-all | bytes 3145728 | tf_op jit(solution)/shard_map/all_to_all | solution.py:185
  30.0 4.3 %shard_map.41 = (f32[8,48,128]{2,1,0:T(8,128)S(1)}, f32[8,48,128]{2,1,0:T(8,128)S(1)}) custom-call(bf16[6144,768]{1,0:T(8,128)(2,1)} %pressures.3, bf16[6144,128]{1,0:T(8,128)(2,1)S(1)} %bitcast.3), custom_call_target="tpu_custom_call" | custom-call | tf_op jit(solution)/shard_map/pallas_call | solution.py:53
  34.4 0.1 collective-permute-start
  34.5 1.4 %collective-permute-done = f32[8,48,128]{2,1,0:T(8,128)S(1)} collective-permute-done((f32[8,48,128]{2,1,0:T(8,128)S(1)}, f32[8,48,128]{2,1,0:T(8,128)S(1)}, u32[]{:S(2)}, u32[]{:S(2)}) %collective-permute-start) | collective-permute-done | bytes 196640 | tf_op jit(solution)/shard_map/ppermute | solution.py:181
  35.9 19.0 %all_to_all.31 = f32[8,48,128]{2,1,0:T(8,128)S(1)} all-to-all(f32[8,48,128]{2,1,0:T(8,128)S(1)} %add.3), channel_id=1, replica_groups={{0,32,64,96,128,160,192,224},{16,48,80,112,144,176,208,240},{1,33,65,97..., dimensions={0} | all-to-all | bytes 393216 | tf_op jit(solution)/shard_map/all_to_all | solution.py:185
  55.0 12.2 %all_to_all.32.mine = f32[8,48,128]{2,1,0:T(8,128)S(1)} all-to-all(f32[8,48,128]{2,1,0:T(8,128)S(1)} %broadcast_in_dim.7), channel_id=1, replica_groups={{0,32,64,96,128,160,192,224},{16,48,80,112,144,176,208,240},{1,33,65,97..., dimensions={0} | all-to-all | bytes 393216 | tf_op jit(solution)/shard_map/all_to_all | solution.py:185
  67.2 0.0 collective-permute-start.1
  67.2 1.4 %collective-permute-done.1.other = f32[8,48,128]{2,1,0:T(8,128)S(1)} collective-permute-done((f32[8,48,128]{2,1,0:T(8,128)S(1)}, f32[8,48,128]{2,1,0:T(8,128)S(1)}, u32[]{:S(2)}, u32[]{:S(2)}) %collective-permute-start.1) | collective-permute-done | bytes 196640 | tf_op jit(solution)/shard_map/ppermute | solution.py:181
  68.6 0.5 shard_map.42
  69.2 8.7 %all_to_all.33 = f32[4,64,128]{2,1,0:T(8,128)S(1)} all-to-all(f32[4,64,128]{2,1,0:T(8,128)S(1)} %get-tuple-element.10), channel_id=1, replica_groups={{0,1,2,3},{4,5,6,7},{8,9,10,11},{12,13,14,15},{16,20,24,28},{17,21,25,2..., dimensions={0} | all-to-all | bytes 262144 | tf_op jit(solution)/shard_map/all_to_all | solution.py:185
  77.9 8.6 %all_to_all.34 = f32[4,64,128]{2,1,0:T(8,128)S(1)} all-to-all(f32[4,64,128]{2,1,0:T(8,128)S(1)} %broadcast_in_dim.8), channel_id=1, replica_groups={{0,4,8,12},{1,5,9,13},{2,6,10,14},{3,7,11,15},{16,17,18,19},{20,21,22,2..., dimensions={0} | all-to-all | bytes 262144 | tf_op jit(solution)/shard_map/all_to_all | solution.py:185
  86.5 0.1 collective-permute-start.2
  86.6 1.2 collective-permute-done.2.other
  87.8 9.7 %shard_map.43 = (bf16[768,128]{1,0:T(8,128)(2,1)}, bf16[6144,128]{1,0:T(8,128)(2,1)S(1)}) custom-call(bf16[6144,768]{1,0:T(8,128)(2,1)} %pressures.3, f32[64,128]{1,0:T(8,128)S(1)} %reduce_sum.38.mine, f32[64,128]{1,0:T(8,128)S(1)} %collective-permute-done.2.other, f32[768,128]{1,0:T(8,128)S(1)} %bitcast.5), custom_call_target="tpu_custom_call" | custom-call | tf_op jit(solution)/shard_map/pallas_call | solution.py:167
  97.5 26.0 %all_to_all.35 = bf16[16,384,128]{2,1,0:T(8,128)(2,1)S(1)} all-to-all(bf16[16,384,128]{2,1,0:T(8,128)(2,1)S(1)} %bitcast.4), channel_id=1, replica_groups=mesh['panel'=16,'tm'=16] {'tm'}, dimensions={0} | all-to-all | bytes 3145728 | tf_op jit(solution)/shard_map/all_to_all | solution.py:185
  123.5 0.9 convert_reduce_fusion
  (6 shorter events, 0.1 us)
Async XLA Ops:
  34.4 1.5 %collective-permute-start = (f32[8,48,128]{2,1,0:T(8,128)S(1)}, f32[8,48,128]{2,1,0:T(8,128)S(1)}, u32[]{:S(2)}, u32[]{:S(2)}) collective-permute-start(f32[8,48,128]{2,1,0:T(8,128)S(1)} %get-tuple-element.9), channel_id=1, source_target_pairs={{0,16},{16,0},{32,48},{48,32},{64,80},{80,64},{96,112},{112,96},{1... | collective-permute-start | bytes 589832 | tf_op jit(solution)/shard_map/ppermute | solution.py:181
  67.2 1.4 %collective-permute-start.1 = (f32[8,48,128]{2,1,0:T(8,128)S(1)}, f32[8,48,128]{2,1,0:T(8,128)S(1)}, u32[]{:S(2)}, u32[]{:S(2)}) collective-permute-start(f32[8,48,128]{2,1,0:T(8,128)S(1)} %all_to_all.32.mine), channel_id=1, source_target_pairs={{0,16},{16,0},{32,48},{48,32},{64,80},{80,64},{96,112},{112,96},{1... | collective-permute-start | bytes 589832 | tf_op jit(solution)/shard_map/ppermute | solution.py:181
  86.5 1.3 %collective-permute-start.2 = (f32[64,128]{1,0:T(8,128)S(1)}, f32[64,128]{1,0:T(8,128)S(1)}, u32[]{:S(2)}, u32[]{:S(2)}) collective-permute-start(f32[64,128]{1,0:T(8,128)S(1)} %reduce_sum.38.mine), channel_id=1, source_target_pairs={{0,16},{16,0},{32,48},{48,32},{64,80},{80,64},{96,112},{112,96},{1... | collective-permute-start | bytes 98312 | tf_op jit(solution)/shard_map/ppermute | solution.py:181

commit v7 on v4

--- a/solution.py
+++ b/solution.py
@@ -10,23 +10,25 @@
 F32 = jnp.float32
 BF16 = jnp.bfloat16
 GROUP = 8
-PIECES = 6
+FOR_PROJECTION = 6
+FOR_IMAGE = 3
 IN_HBM = pl.BlockSpec(memory_space=pltpu.HBM)
 IN_VMEM = pl.BlockSpec(memory_space=pltpu.VMEM)
 ROOM = pltpu.CompilerParams(vmem_limit_bytes=32 << 20)
 
 
 def fetch(pressures, held, arrived):
-    rows = held.shape[0] // PIECES
-    parts = [pl.ds(i * rows, rows) for i in range(PIECES)]
+    pieces = arrived.shape[0]
+    rows = held.shape[0] // pieces
+    parts = [pl.ds(i * rows, rows) for i in range(pieces)]
     copies = [pltpu.make_async_copy(pressures.at[r], held.at[r], arrived.at[i]) for i, r in enumerate(parts)]
     for copy in copies:
         copy.start()
     return list(zip(copies, parts))
 
 
-def held_like(pressures):
-    return [pltpu.VMEM(pressures.shape, pressures.dtype), pltpu.SemaphoreType.DMA((PIECES,))]
+def held_like(pressures, pieces):
+    return [pltpu.VMEM(pressures.shape, pressures.dtype), pltpu.SemaphoreType.DMA((pieces,))]
 
 
 def own_core():
@@ -55,7 +57,7 @@
         out_shape=(half, half),
         in_specs=[IN_HBM, IN_VMEM],
         out_specs=(IN_VMEM, IN_VMEM),
-        scratch_shapes=held_like(pressures),
+        scratch_shapes=held_like(pressures, FOR_PROJECTION),
         compiler_params=ROOM,
     )(pressures, sketch)
 
@@ -168,7 +170,7 @@
         ),
         in_specs=[IN_HBM, IN_VMEM, IN_VMEM],
         out_specs=(IN_VMEM, IN_VMEM),
-        scratch_shapes=[*held_like(pressures), pltpu.VMEM((modes, modes), F32)],
+        scratch_shapes=[*held_like(pressures, FOR_IMAGE), pltpu.VMEM((modes, modes), F32)],
         compiler_params=ROOM,
     )(pressures, gram_parts, y_rows)
 

time: 123 us -> 122 us (level)
  no operation moved by 1% of the time
where the time goes in v7:
time: 122 us
  blocking collectives  102 us (84%)
  Pallas kernels  14 us (11%)
  waiting for transfers between devices  2.87 us (2%)
  local copies, waits for them, and re-layouts  1.22 us (1%)
    all_to_all x6, blocking collectives, exchange(): return lax.all_to_all(x, axis, 0, 0, axis_index_groups=groups)  102 us
    pallas_call x1, Pallas kernels, basis_and_image(): pl.pallas_call(image_kernel, out_shape=(jax.ShapeDtypeStruct((samples, mo...  9.1 us
    pallas_call x1, Pallas kernels, projection(): pl.pallas_call(projection_kernel, out_shape=(half, half), in_specs=[IN_HB...  4.32 us
    ppermute x2, waiting for transfers between devices, swap_cores(): lax.ppermute(x, 'panel', [(i, i ^ 1) for i in range(lax.axis_size('panel'...  2.87 us
  transfers between devices with their start and end apart: 2, of which 2 were waited for; matrix products, arithmetic and copies ran while one was open for 0% of the time, Pallas kernels for 0%

profile of v7, /device:TPU:8, one launch (start us, length us, event | category | flops | bytes accessed | tf_op | source)
XLA Modules:
  0.0 122.0 jit_solution(14700343871567062827)
XLA Ops:
  0.6 1.2 broadcast_in_dim.6
  1.8 28.2 %all_to_all.30 = bf16[16,384,128]{2,1,0:T(8,128)(2,1)S(1)} all-to-all(bf16[16,384,128]{2,1,0:T(8,128)(2,1)S(1)} %broadcast_in_dim.6), channel_id=1, replica_groups=mesh['panel'=16,'tm'=16] {'tm'}, dimensions={0} | all-to-all | bytes 3145728 | tf_op jit(solution)/shard_map/all_to_all | solution.py:183
  30.0 4.3 %shard_map.41 = (f32[8,48,128]{2,1,0:T(8,128)S(1)}, f32[8,48,128]{2,1,0:T(8,128)S(1)}) custom-call(bf16[6144,768]{1,0:T(8,128)(2,1)} %pressures.3, bf16[6144,128]{1,0:T(8,128)(2,1)S(1)} %bitcast.3), custom_call_target="tpu_custom_call" | custom-call | tf_op jit(solution)/shard_map/pallas_call | solution.py:55
  34.4 0.1 collective-permute-start
  34.5 1.4 %collective-permute-done = f32[8,48,128]{2,1,0:T(8,128)S(1)} collective-permute-done((f32[8,48,128]{2,1,0:T(8,128)S(1)}, f32[8,48,128]{2,1,0:T(8,128)S(1)}, u32[]{:S(2)}, u32[]{:S(2)}) %collective-permute-start) | collective-permute-done | bytes 196640 | tf_op jit(solution)/shard_map/ppermute | solution.py:179
  35.9 19.0 %all_to_all.31 = f32[8,48,128]{2,1,0:T(8,128)S(1)} all-to-all(f32[8,48,128]{2,1,0:T(8,128)S(1)} %add.3), channel_id=1, replica_groups={{0,32,64,96,128,160,192,224},{16,48,80,112,144,176,208,240},{1,33,65,97..., dimensions={0} | all-to-all | bytes 393216 | tf_op jit(solution)/shard_map/all_to_all | solution.py:183
  55.0 12.2 %all_to_all.32.mine = f32[8,48,128]{2,1,0:T(8,128)S(1)} all-to-all(f32[8,48,128]{2,1,0:T(8,128)S(1)} %broadcast_in_dim.7), channel_id=1, replica_groups={{0,32,64,96,128,160,192,224},{16,48,80,112,144,176,208,240},{1,33,65,97..., dimensions={0} | all-to-all | bytes 393216 | tf_op jit(solution)/shard_map/all_to_all | solution.py:183
  67.2 0.0 collective-permute-start.1
  67.2 1.4 %collective-permute-done.1.other = f32[8,48,128]{2,1,0:T(8,128)S(1)} collective-permute-done((f32[8,48,128]{2,1,0:T(8,128)S(1)}, f32[8,48,128]{2,1,0:T(8,128)S(1)}, u32[]{:S(2)}, u32[]{:S(2)}) %collective-permute-start.1) | collective-permute-done | bytes 196640 | tf_op jit(solution)/shard_map/ppermute | solution.py:179
  68.6 0.5 shard_map.42
  69.1 9.8 %all_to_all.33 = f32[4,128,128]{2,1,0:T(8,128)S(1)} all-to-all(f32[4,128,128]{2,1,0:T(8,128)S(1)} %get-tuple-element.10), channel_id=1, replica_groups={{0,1,2,3},{4,5,6,7},{8,9,10,11},{12,13,14,15},{16,17,18,19},{20,21,22,2..., dimensions={0} | all-to-all | bytes 524288 | tf_op jit(solution)/shard_map/all_to_all | solution.py:183
  79.0 9.2 %all_to_all.34.gram_parts = f32[4,128,128]{2,1,0:T(8,128)S(1)} all-to-all(f32[4,128,128]{2,1,0:T(8,128)S(1)} %broadcast_in_dim.8), channel_id=1, replica_groups={{0,4,8,12},{1,5,9,13},{2,6,10,14},{3,7,11,15},{16,20,24,28},{17,21,25,2..., dimensions={0} | all-to-all | bytes 524288 | tf_op jit(solution)/shard_map/all_to_all | solution.py:183
  88.2 9.1 %shard_map.43 = (bf16[768,128]{1,0:T(8,128)(2,1)}, bf16[6144,128]{1,0:T(8,128)(2,1)S(1)}) custom-call(bf16[6144,768]{1,0:T(8,128)(2,1)} %pressures.3, f32[4,128,128]{2,1,0:T(8,128)S(1)} %all_to_all.34.gram_parts, f32[768,128]{1,0:T(8,128)S(1)} %bitcast.5), custom_call_target="tpu_custom_call" | custom-call | tf_op jit(solution)/shard_map/pallas_call | solution.py:165
  97.3 23.8 %all_to_all.35 = bf16[16,384,128]{2,1,0:T(8,128)(2,1)S(1)} all-to-all(bf16[16,384,128]{2,1,0:T(8,128)(2,1)S(1)} %bitcast.4), channel_id=1, replica_groups=mesh['panel'=16,'tm'=16] {'tm'}, dimensions={0} | all-to-all | bytes 3145728 | tf_op jit(solution)/shard_map/all_to_all | solution.py:183
  121.1 0.9 convert_reduce_fusion
  (5 shorter events, 0.1 us)
Async XLA Ops:
  34.4 1.5 %collective-permute-start = (f32[8,48,128]{2,1,0:T(8,128)S(1)}, f32[8,48,128]{2,1,0:T(8,128)S(1)}, u32[]{:S(2)}, u32[]{:S(2)}) collective-permute-start(f32[8,48,128]{2,1,0:T(8,128)S(1)} %get-tuple-element.9), channel_id=1, source_target_pairs={{0,16},{16,0},{32,48},{48,32},{64,80},{80,64},{96,112},{112,96},{1... | collective-permute-start | bytes 589832 | tf_op jit(solution)/shard_map/ppermute | solution.py:179
  67.2 1.4 %collective-permute-start.1 = (f32[8,48,128]{2,1,0:T(8,128)S(1)}, f32[8,48,128]{2,1,0:T(8,128)S(1)}, u32[]{:S(2)}, u32[]{:S(2)}) collective-permute-start(f32[8,48,128]{2,1,0:T(8,128)S(1)} %all_to_all.32.mine), channel_id=1, source_target_pairs={{0,16},{16,0},{32,48},{48,32},{64,80},{80,64},{96,112},{112,96},{1... | collective-permute-start | bytes 589832 | tf_op jit(solution)/shard_map/ppermute | solution.py:179

commit v8 on v7

--- a/solution.py
+++ b/solution.py
@@ -10,25 +10,24 @@
 F32 = jnp.float32
 BF16 = jnp.bfloat16
 GROUP = 8
-FOR_PROJECTION = 6
-FOR_IMAGE = 3
+FOR_PROJECTION = (4, 4, 3, 1)
+FOR_IMAGE = (1, 1, 1)
 IN_HBM = pl.BlockSpec(memory_space=pltpu.HBM)
 IN_VMEM = pl.BlockSpec(memory_space=pltpu.VMEM)
 ROOM = pltpu.CompilerParams(vmem_limit_bytes=32 << 20)
 
 
-def fetch(pressures, held, arrived):
-    pieces = arrived.shape[0]
-    rows = held.shape[0] // pieces
-    parts = [pl.ds(i * rows, rows) for i in range(pieces)]
+def fetch(pressures, held, arrived, shares):
+    unit = held.shape[0] // sum(shares)
+    parts = [pl.ds(sum(shares[:i]) * unit, share * unit) for i, share in enumerate(shares)]
     copies = [pltpu.make_async_copy(pressures.at[r], held.at[r], arrived.at[i]) for i, r in enumerate(parts)]
     for copy in copies:
         copy.start()
     return list(zip(copies, parts))
 
 
-def held_like(pressures, pieces):
-    return [pltpu.VMEM(pressures.shape, pressures.dtype), pltpu.SemaphoreType.DMA((pieces,))]
+def held_like(pressures, shares):
+    return [pltpu.VMEM(pressures.shape, pressures.dtype), pltpu.SemaphoreType.DMA((len(shares),))]
 
 
 def own_core():
@@ -37,7 +36,7 @@
 
 def projection_kernel(pressures, sketch, keep_ref, give_ref, held, arrived):
     total = None
-    for copy, r in fetch(pressures, held, arrived):
+    for copy, r in fetch(pressures, held, arrived, FOR_PROJECTION):
         copy.wait()
         term = lax.dot_general(sketch[r, :], held[r, :], (((0,), (0,)), ((), ())), preferred_element_type=F32)
         total = term if total is None else total + term
@@ -143,7 +142,7 @@
 
 
 def image_kernel(pressures, gram_parts, y_ref, basis_ref, image_ref, held, arrived, inverse):
-    arriving = fetch(pressures, held, arrived)
+    arriving = fetch(pressures, held, arrived, FOR_IMAGE)
     for i, rows in enumerate(inverse_factor(jnp.sum(gram_parts[...], axis=0))):
         inverse[GROUP * i : GROUP * (i + 1), :] = rows
     basis = lax.dot_general(

time: 122 us -> 123 us (level)
  no operation moved by 1% of the time
where the time goes in v8:
time: 123 us; the launch traced here: 122 us
  blocking collectives  102 us (83%)
  Pallas kernels  14.4 us (12%)
  waiting for transfers between devices  2.87 us (2%)
    all_to_all x6, blocking collectives, exchange(): return lax.all_to_all(x, axis, 0, 0, axis_index_groups=groups)  102 us
    pallas_call x1, Pallas kernels, basis_and_image(): pl.pallas_call(image_kernel, out_shape=(jax.ShapeDtypeStruct((samples, mo...  9.1 us
    pallas_call x1, Pallas kernels, projection(): pl.pallas_call(projection_kernel, out_shape=(half, half), in_specs=[IN_HB...  4.78 us
    ppermute x2, waiting for transfers between devices, swap_cores(): lax.ppermute(x, 'panel', [(i, i ^ 1) for i in range(lax.axis_size('panel'...  2.87 us
  transfers between devices with their start and end apart: 2, of which 2 were waited for; matrix products, arithmetic and copies ran while one was open for 0% of the time, Pallas kernels for 0%

profile of v8, /device:TPU:8, one launch (start us, length us, event | category | flops | bytes accessed | tf_op | source)
XLA Modules:
  0.0 122.4 jit_solution(8302423864430738802)
XLA Ops:
  0.6 1.2 broadcast_in_dim.6
  1.8 28.2 %all_to_all.30 = bf16[16,384,128]{2,1,0:T(8,128)(2,1)S(1)} all-to-all(bf16[16,384,128]{2,1,0:T(8,128)(2,1)S(1)} %broadcast_in_dim.6), channel_id=1, replica_groups=mesh['panel'=16,'tm'=16] {'tm'}, dimensions={0} | all-to-all | bytes 3145728 | tf_op jit(solution)/shard_map/all_to_all | solution.py:182
  30.0 4.8 %shard_map.41 = (f32[8,48,128]{2,1,0:T(8,128)S(1)}, f32[8,48,128]{2,1,0:T(8,128)S(1)}) custom-call(bf16[6144,768]{1,0:T(8,128)(2,1)} %pressures.3, bf16[6144,128]{1,0:T(8,128)(2,1)S(1)} %bitcast.3), custom_call_target="tpu_custom_call" | custom-call | tf_op jit(solution)/shard_map/pallas_call | solution.py:54
  34.8 0.1 collective-permute-start
  34.9 1.4 %collective-permute-done = f32[8,48,128]{2,1,0:T(8,128)S(1)} collective-permute-done((f32[8,48,128]{2,1,0:T(8,128)S(1)}, f32[8,48,128]{2,1,0:T(8,128)S(1)}, u32[]{:S(2)}, u32[]{:S(2)}) %collective-permute-start) | collective-permute-done | bytes 196640 | tf_op jit(solution)/shard_map/ppermute | solution.py:178
  36.4 19.0 %all_to_all.31 = f32[8,48,128]{2,1,0:T(8,128)S(1)} all-to-all(f32[8,48,128]{2,1,0:T(8,128)S(1)} %add.3), channel_id=1, replica_groups={{0,32,64,96,128,160,192,224},{16,48,80,112,144,176,208,240},{1,33,65,97..., dimensions={0} | all-to-all | bytes 393216 | tf_op jit(solution)/shard_map/all_to_all | solution.py:182
  55.4 12.2 %all_to_all.32.mine = f32[8,48,128]{2,1,0:T(8,128)S(1)} all-to-all(f32[8,48,128]{2,1,0:T(8,128)S(1)} %broadcast_in_dim.7), channel_id=1, replica_groups={{0,32,64,96,128,160,192,224},{16,48,80,112,144,176,208,240},{1,33,65,97..., dimensions={0} | all-to-all | bytes 393216 | tf_op jit(solution)/shard_map/all_to_all | solution.py:182
  67.6 0.0 collective-permute-start.1
  67.6 1.4 %collective-permute-done.1.other = f32[8,48,128]{2,1,0:T(8,128)S(1)} collective-permute-done((f32[8,48,128]{2,1,0:T(8,128)S(1)}, f32[8,48,128]{2,1,0:T(8,128)S(1)}, u32[]{:S(2)}, u32[]{:S(2)}) %collective-permute-start.1) | collective-permute-done | bytes 196640 | tf_op jit(solution)/shard_map/ppermute | solution.py:178
  69.1 0.5 shard_map.42
  69.6 9.8 %all_to_all.33 = f32[4,128,128]{2,1,0:T(8,128)S(1)} all-to-all(f32[4,128,128]{2,1,0:T(8,128)S(1)} %get-tuple-element.10), channel_id=1, replica_groups={{0,1,2,3},{4,5,6,7},{8,9,10,11},{12,13,14,15},{16,17,18,19},{20,21,22,2..., dimensions={0} | all-to-all | bytes 524288 | tf_op jit(solution)/shard_map/all_to_all | solution.py:182
  79.5 9.2 %all_to_all.34.gram_parts = f32[4,128,128]{2,1,0:T(8,128)S(1)} all-to-all(f32[4,128,128]{2,1,0:T(8,128)S(1)} %broadcast_in_dim.8), channel_id=1, replica_groups={{0,4,8,12},{1,5,9,13},{2,6,10,14},{3,7,11,15},{16,20,24,28},{17,21,25,2..., dimensions={0} | all-to-all | bytes 524288 | tf_op jit(solution)/shard_map/all_to_all | solution.py:182
  88.7 9.1 %shard_map.43 = (bf16[768,128]{1,0:T(8,128)(2,1)}, bf16[6144,128]{1,0:T(8,128)(2,1)S(1)}) custom-call(bf16[6144,768]{1,0:T(8,128)(2,1)} %pressures.3, f32[4,128,128]{2,1,0:T(8,128)S(1)} %all_to_all.34.gram_parts, f32[768,128]{1,0:T(8,128)S(1)} %bitcast.5), custom_call_target="tpu_custom_call" | custom-call | tf_op jit(solution)/shard_map/pallas_call | solution.py:164
  97.8 23.8 %all_to_all.35 = bf16[16,384,128]{2,1,0:T(8,128)(2,1)S(1)} all-to-all(bf16[16,384,128]{2,1,0:T(8,128)(2,1)S(1)} %bitcast.4), channel_id=1, replica_groups=mesh['panel'=16,'tm'=16] {'tm'}, dimensions={0} | all-to-all | bytes 3145728 | tf_op jit(solution)/shard_map/all_to_all | solution.py:182
  121.5 0.9 convert_reduce_fusion
  (5 shorter events, 0.1 us)
Async XLA Ops:
  34.8 1.5 %collective-permute-start = (f32[8,48,128]{2,1,0:T(8,128)S(1)}, f32[8,48,128]{2,1,0:T(8,128)S(1)}, u32[]{:S(2)}, u32[]{:S(2)}) collective-permute-start(f32[8,48,128]{2,1,0:T(8,128)S(1)} %get-tuple-element.9), channel_id=1, source_target_pairs={{0,16},{16,0},{32,48},{48,32},{64,80},{80,64},{96,112},{112,96},{1... | collective-permute-start | bytes 589832 | tf_op jit(solution)/shard_map/ppermute | solution.py:178
  67.6 1.4 %collective-permute-start.1 = (f32[8,48,128]{2,1,0:T(8,128)S(1)}, f32[8,48,128]{2,1,0:T(8,128)S(1)}, u32[]{:S(2)}, u32[]{:S(2)}) collective-permute-start(f32[8,48,128]{2,1,0:T(8,128)S(1)} %all_to_all.32.mine), channel_id=1, source_target_pairs={{0,16},{16,0},{32,48},{48,32},{64,80},{80,64},{96,112},{112,96},{1... | collective-permute-start | bytes 589832 | tf_op jit(solution)/shard_map/ppermute | solution.py:178

commit v9 on v7

--- a/solution.py
+++ b/solution.py
@@ -10,7 +10,7 @@
 F32 = jnp.float32
 BF16 = jnp.bfloat16
 GROUP = 8
-FOR_PROJECTION = 6
+FOR_PROJECTION = 4
 FOR_IMAGE = 3
 IN_HBM = pl.BlockSpec(memory_space=pltpu.HBM)
 IN_VMEM = pl.BlockSpec(memory_space=pltpu.VMEM)

time: 122 us -> 122 us (level)
  no operation moved by 1% of the time
where the time goes in v9:
time: 122 us
  blocking collectives  102 us (84%)
  Pallas kernels  14.1 us (12%)
  waiting for transfers between devices  2.87 us (2%)
  local copies, waits for them, and re-layouts  1.22 us (1%)
    all_to_all x6, blocking collectives, exchange(): return lax.all_to_all(x, axis, 0, 0, axis_index_groups=groups)  102 us
    pallas_call x1, Pallas kernels, basis_and_image(): pl.pallas_call(image_kernel, out_shape=(jax.ShapeDtypeStruct((samples, mo...  9.11 us
    pallas_call x1, Pallas kernels, projection(): pl.pallas_call(projection_kernel, out_shape=(half, half), in_specs=[IN_HB...  4.48 us
    ppermute x2, waiting for transfers between devices, swap_cores(): lax.ppermute(x, 'panel', [(i, i ^ 1) for i in range(lax.axis_size('panel'...  2.87 us
  transfers between devices with their start and end apart: 2, of which 2 were waited for; matrix products, arithmetic and copies ran while one was open for 0% of the time, Pallas kernels for 0%

profile of v9, /device:TPU:8, one launch (start us, length us, event | category | flops | bytes accessed | tf_op | source)
XLA Modules:
  0.0 122.2 jit_solution(12472013301801181423)
XLA Ops:
  0.6 1.2 broadcast_in_dim.6
  1.8 28.2 %all_to_all.30 = bf16[16,384,128]{2,1,0:T(8,128)(2,1)S(1)} all-to-all(bf16[16,384,128]{2,1,0:T(8,128)(2,1)S(1)} %broadcast_in_dim.6), channel_id=1, replica_groups=mesh['panel'=16,'tm'=16] {'tm'}, dimensions={0} | all-to-all | bytes 3145728 | tf_op jit(solution)/shard_map/all_to_all | solution.py:183
  30.0 4.5 %shard_map.41 = (f32[8,48,128]{2,1,0:T(8,128)S(1)}, f32[8,48,128]{2,1,0:T(8,128)S(1)}) custom-call(bf16[6144,768]{1,0:T(8,128)(2,1)} %pressures.3, bf16[6144,128]{1,0:T(8,128)(2,1)S(1)} %bitcast.3), custom_call_target="tpu_custom_call" | custom-call | tf_op jit(solution)/shard_map/pallas_call | solution.py:55
  34.5 0.1 collective-permute-start
  34.6 1.4 %collective-permute-done = f32[8,48,128]{2,1,0:T(8,128)S(1)} collective-permute-done((f32[8,48,128]{2,1,0:T(8,128)S(1)}, f32[8,48,128]{2,1,0:T(8,128)S(1)}, u32[]{:S(2)}, u32[]{:S(2)}) %collective-permute-start) | collective-permute-done | bytes 196640 | tf_op jit(solution)/shard_map/ppermute | solution.py:179
  36.1 19.0 %all_to_all.31 = f32[8,48,128]{2,1,0:T(8,128)S(1)} all-to-all(f32[8,48,128]{2,1,0:T(8,128)S(1)} %add.3), channel_id=1, replica_groups={{0,32,64,96,128,160,192,224},{16,48,80,112,144,176,208,240},{1,33,65,97..., dimensions={0} | all-to-all | bytes 393216 | tf_op jit(solution)/shard_map/all_to_all | solution.py:183
  55.2 12.2 %all_to_all.32.mine = f32[8,48,128]{2,1,0:T(8,128)S(1)} all-to-all(f32[8,48,128]{2,1,0:T(8,128)S(1)} %broadcast_in_dim.7), channel_id=1, replica_groups={{0,32,64,96,128,160,192,224},{16,48,80,112,144,176,208,240},{1,33,65,97..., dimensions={0} | all-to-all | bytes 393216 | tf_op jit(solution)/shard_map/all_to_all | solution.py:183
  67.3 0.0 collective-permute-start.1
  67.3 1.4 %collective-permute-done.1.other = f32[8,48,128]{2,1,0:T(8,128)S(1)} collective-permute-done((f32[8,48,128]{2,1,0:T(8,128)S(1)}, f32[8,48,128]{2,1,0:T(8,128)S(1)}, u32[]{:S(2)}, u32[]{:S(2)}) %collective-permute-start.1) | collective-permute-done | bytes 196640 | tf_op jit(solution)/shard_map/ppermute | solution.py:179
  68.8 0.5 shard_map.42
  69.3 9.8 %all_to_all.33 = f32[4,128,128]{2,1,0:T(8,128)S(1)} all-to-all(f32[4,128,128]{2,1,0:T(8,128)S(1)} %get-tuple-element.10), channel_id=1, replica_groups={{0,1,2,3},{4,5,6,7},{8,9,10,11},{12,13,14,15},{16,17,18,19},{20,21,22,2..., dimensions={0} | all-to-all | bytes 524288 | tf_op jit(solution)/shard_map/all_to_all | solution.py:183
  79.2 9.2 %all_to_all.34.gram_parts = f32[4,128,128]{2,1,0:T(8,128)S(1)} all-to-all(f32[4,128,128]{2,1,0:T(8,128)S(1)} %broadcast_in_dim.8), channel_id=1, replica_groups={{0,4,8,12},{1,5,9,13},{2,6,10,14},{3,7,11,15},{16,20,24,28},{17,21,25,2..., dimensions={0} | all-to-all | bytes 524288 | tf_op jit(solution)/shard_map/all_to_all | solution.py:183
  88.4 9.1 %shard_map.43 = (bf16[768,128]{1,0:T(8,128)(2,1)}, bf16[6144,128]{1,0:T(8,128)(2,1)S(1)}) custom-call(bf16[6144,768]{1,0:T(8,128)(2,1)} %pressures.3, f32[4,128,128]{2,1,0:T(8,128)S(1)} %all_to_all.34.gram_parts, f32[768,128]{1,0:T(8,128)S(1)} %bitcast.5), custom_call_target="tpu_custom_call" | custom-call | tf_op jit(solution)/shard_map/pallas_call | solution.py:165
  97.5 23.8 %all_to_all.35 = bf16[16,384,128]{2,1,0:T(8,128)(2,1)S(1)} all-to-all(bf16[16,384,128]{2,1,0:T(8,128)(2,1)S(1)} %bitcast.4), channel_id=1, replica_groups=mesh['panel'=16,'tm'=16] {'tm'}, dimensions={0} | all-to-all | bytes 3145728 | tf_op jit(solution)/shard_map/all_to_all | solution.py:183
  121.3 0.9 convert_reduce_fusion
  (5 shorter events, 0.1 us)
Async XLA Ops:
  34.5 1.5 %collective-permute-start = (f32[8,48,128]{2,1,0:T(8,128)S(1)}, f32[8,48,128]{2,1,0:T(8,128)S(1)}, u32[]{:S(2)}, u32[]{:S(2)}) collective-permute-start(f32[8,48,128]{2,1,0:T(8,128)S(1)} %get-tuple-element.9), channel_id=1, source_target_pairs={{0,16},{16,0},{32,48},{48,32},{64,80},{80,64},{96,112},{112,96},{1... | collective-permute-start | bytes 589832 | tf_op jit(solution)/shard_map/ppermute | solution.py:179
  67.3 1.4 %collective-permute-start.1 = (f32[8,48,128]{2,1,0:T(8,128)S(1)}, f32[8,48,128]{2,1,0:T(8,128)S(1)}, u32[]{:S(2)}, u32[]{:S(2)}) collective-permute-start(f32[8,48,128]{2,1,0:T(8,128)S(1)} %all_to_all.32.mine), channel_id=1, source_target_pairs={{0,16},{16,0},{32,48},{48,32},{64,80},{80,64},{96,112},{112,96},{1... | collective-permute-start | bytes 589832 | tf_op jit(solution)/shard_map/ppermute | solution.py:179
